TPU v7x, 256 devices: a whole 4x4x8 slice. The times are simulated.
256 devices in a mesh: group: 4 (over y_hi, core), member: 64 (over z, y_lo, x).
Axes of the slice: x: 4, y: 4 (y_hi: 2, y_lo: 2; y = y_hi * 2 + y_lo), z: 8, core: 2. Of those that a mesh axis runs over, the one named last changes fastest.
Arguments:
- coefficients: float32 [2048, 3, 289], P(('group', 'member')), may hold values from -2.5 to 2.5
- pair_list: int32 [4096, 2], P(('group', 'member')), may hold values from -1 to 2047, as said below
- pair_offset: float32 [4096, 3], P(('group', 'member')), may hold values from -2.6 to 2.6
Outputs:
- force_coef: float32 [2048, 3, 289], P(('group', 'member'))
Inputs may be any that keep to these rules, and one draw needn't show every extreme that they name: `pair_list`: each row is (i, j) or (-1, -1) for an empty slot; on every device the live rows come first and some device has all 16 rows live. i is owned by a device of the pair owner's group; j is too, or else j is one of the first 4 vesicles of the device with the same member index in an adjacent group. Of one device's in-group entries (i and j), at most 2 are owned by any one device, and the full device reaches 2.
All inputs are finite; a program needn't handle non-finite values.
Results may differ from a plain program's by a relative error of at most 0.0003.
Values sent between devices are 32-bit elements; how exact they have to be, the bound alone decides.
No kernel may reach another device: no remote copies, remote signals or barrier semaphores. Data moves between devices by JAX's collectives and lax.ppermute only.
A program may use at most 64 MiB of HBM per device.

v0:
```python
import math

import jax
import jax.numpy as jnp
from jax import lax
from jax.sharding import PartitionSpec as P

ORDER = 16
UPORDER = 32
RIM_VES = 4


def extended(block, sides, width):
    for axis, dim in sides:
        count = lax.axis_size(axis)
        forward = [(i, i + 1) for i in range(count - 1)]
        backward = [(target, source) for source, target in forward]
        low = lax.ppermute(
            lax.slice_in_dim(block, block.shape[dim] - width, None, axis=dim), axis, forward
        )
        high = lax.ppermute(lax.slice_in_dim(block, 0, width, axis=dim), axis, backward)
        block = jnp.concatenate([low, block, high], axis=dim)
    return block


def contact_width(up_order):
    return (0.7 * math.pi / (up_order + 1)) ** 2


def legendre_table(order_max, cosine, sine_theta):
    legendre = {}
    diagonal = jnp.ones_like(cosine) * math.sqrt(1.0 / (4.0 * math.pi))
    for azimuth in range(order_max + 1):
        if azimuth > 0:
            diagonal = -math.sqrt((2.0 * azimuth + 1.0) / (2.0 * azimuth)) * sine_theta * diagonal
        legendre[azimuth, azimuth] = diagonal
        if azimuth < order_max:
            legendre[azimuth + 1, azimuth] = math.sqrt(2.0 * azimuth + 3.0) * cosine * diagonal
        for degree in range(azimuth + 2, order_max + 1):
            factor_one = math.sqrt(
                (4.0 * degree * degree - 1.0) / (degree * degree - azimuth * azimuth)
            )
            factor_two = math.sqrt(
                ((degree - 1.0) ** 2 - azimuth * azimuth) / (4.0 * (degree - 1.0) ** 2 - 1.0)
            )
            legendre[degree, azimuth] = factor_one * (
                cosine * legendre[degree - 1, azimuth] - factor_two * legendre[degree - 2, azimuth]
            )
    return legendre


def basis_table(order_max, up_order):
    lat_count = up_order + 1
    lon_count = 2 * up_order
    polar_angle = (jnp.arange(lat_count, dtype=jnp.float32) + 0.5) * (math.pi / lat_count)
    longitude = jnp.arange(lon_count, dtype=jnp.float32) * (2.0 * math.pi / lon_count)
    cosine = jnp.cos(polar_angle)
    sine_theta = jnp.sin(polar_angle)
    legendre = legendre_table(order_max, cosine, sine_theta)
    ones_row = jnp.ones_like(longitude)
    basis_rows = []
    for degree in range(order_max + 1):
        for azimuth in range(-degree, degree + 1):
            if azimuth == 0:
                beside_all = ones_row
            elif azimuth > 0:
                beside_all = math.sqrt(2.0) * jnp.cos(azimuth * longitude)
            else:
                beside_all = math.sqrt(2.0) * jnp.sin(-azimuth * longitude)
            basis_rows.append(
                (legendre[degree, abs(azimuth)][:, None] * beside_all[None, :]).reshape(-1)
            )
    harmonics = jnp.stack(basis_rows)
    weights = (
        (sine_theta[:, None] * ones_row[None, :]).reshape(-1)
        * (math.pi / lat_count)
        * (2.0 * math.pi / lon_count)
    )
    return (harmonics, weights)


def upsample(coef_block, harmonics):
    vesicle_count = coef_block.shape[0]
    surface = jnp.dot(
        coef_block.reshape(vesicle_count * 3, -1),
        harmonics,
        precision=lax.Precision.HIGHEST,
        preferred_element_type=jnp.float32,
    )
    return surface.reshape(vesicle_count, 3, -1)


def project(point_force, harmonics, weights):
    vesicle_count = point_force.shape[0]
    weighted = (point_force * weights[None, None, :]).reshape(vesicle_count * 3, -1)
    result = jnp.dot(
        weighted, harmonics.T, precision=lax.Precision.HIGHEST, preferred_element_type=jnp.float32
    )
    return result.reshape(vesicle_count, 3, -1)


def pair_forces(near_side, far_side, width):
    points = near_side.shape[1]
    blocks = max(1, points // 512)
    block_width = points // blocks
    factor = 1.0 / (points * width * width)
    near_parts = []
    far_total = jnp.zeros((3, points), jnp.float32)
    for block_index in range(blocks):
        near_block = near_side[:, block_index * block_width : (block_index + 1) * block_width]
        delta_x = near_block[0][:, None] - far_side[0][None, :]
        delta_y = near_block[1][:, None] - far_side[1][None, :]
        delta_z = near_block[2][:, None] - far_side[2][None, :]
        dist_sq = delta_x * delta_x + delta_y * delta_y + delta_z * delta_z
        kernel = 1.0 / (1.0 + dist_sq / width)
        kernel = kernel * kernel
        near_parts.append(
            jnp.stack(
                [
                    jnp.sum(kernel * delta_x, axis=1),
                    jnp.sum(kernel * delta_y, axis=1),
                    jnp.sum(kernel * delta_z, axis=1),
                ]
            )
        )
        far_total = far_total + jnp.stack(
            [
                jnp.sum(kernel * delta_x, axis=0),
                jnp.sum(kernel * delta_y, axis=0),
                jnp.sum(kernel * delta_z, axis=0),
            ]
        )
    return (jnp.concatenate(near_parts, axis=1) * factor, -far_total * factor)


def per_device(coefficients, pair_list, pair_offset):
    members = lax.axis_size("member")
    group_here = lax.axis_index("group")
    vesicle_count = coefficients.shape[0]
    pair_count = pair_list.shape[0]
    slot_cap = max(2, (2 * pair_count + members - 1) // members)
    total_slots = members * slot_cap
    harmonics, weights = basis_table(ORDER, UPORDER)
    width = contact_width(UPORDER)
    points = harmonics.shape[1]
    end_ids = pair_list.reshape(-1)
    end_live = end_ids >= 0
    safe_ids = jnp.maximum(end_ids, 0)
    owner_device = safe_ids // vesicle_count
    owner_group = owner_device // members
    owner_member = owner_device % members
    owner_slot = safe_ids % vesicle_count
    inside = end_live & (owner_group == group_here)
    member_hits = (
        (owner_member[:, None] == jnp.arange(members)[None, :]) & inside[:, None]
    ).astype(jnp.int32)
    earlier = jnp.sum((jnp.cumsum(member_hits, axis=0) - member_hits) * member_hits, axis=1)
    end_slot = jnp.where(inside, owner_member * slot_cap + earlier, total_slots)
    request = jnp.full((total_slots + 1,), -1, jnp.int32).at[end_slot].set(owner_slot)[:total_slots]
    asked_for = lax.all_to_all(
        request.reshape(members, slot_cap), "member", split_axis=0, concat_axis=0, tiled=True
    ).reshape(-1)
    asked_valid = asked_for >= 0
    asked_safe = jnp.maximum(asked_for, 0)
    local_surface = upsample(coefficients, harmonics)
    outgoing = jnp.where(asked_valid[:, None, None], local_surface[asked_safe], 0.0)
    received = lax.all_to_all(
        outgoing.reshape(members, slot_cap, 3, points),
        "member",
        split_axis=0,
        concat_axis=0,
        tiled=True,
    ).reshape(total_slots, 3, points)
    rim_surface = local_surface[:RIM_VES]
    ghosts = extended(rim_surface, (("group", 0),), RIM_VES)
    ghost_row = jnp.clip((owner_group - group_here + 1) * RIM_VES + owner_slot, 0, 3 * RIM_VES - 1)
    return_row = jnp.where(
        inside,
        2 * RIM_VES,
        jnp.where(owner_group < group_here, 0, RIM_VES) + jnp.minimum(owner_slot, RIM_VES - 1),
    )
    live_pairs = jnp.sum(end_live.astype(jnp.int32)) // 2

    def add_pair(pair_index, state_pair):
        slot_force, rim_force = state_pair
        near_end = 2 * pair_index
        far_end = near_end + 1
        offset_row = lax.dynamic_index_in_dim(pair_offset, pair_index, 0, keepdims=False)
        near_side = (
            lax.dynamic_index_in_dim(received, end_slot[near_end], 0, keepdims=False)
            + offset_row[:, None]
        )
        far_slot = jnp.minimum(end_slot[far_end], total_slots - 1)
        far_inside = lax.dynamic_index_in_dim(received, far_slot, 0, keepdims=False)
        far_ghost = lax.dynamic_index_in_dim(ghosts, ghost_row[far_end], 0, keepdims=False)
        far_side = jnp.where(inside[far_end], far_inside, far_ghost)
        on_near, on_far = pair_forces(near_side, far_side, width)
        slot_force = lax.dynamic_update_index_in_dim(slot_force, on_near, end_slot[near_end], 0)
        slot_force = lax.dynamic_update_index_in_dim(slot_force, on_far, end_slot[far_end], 0)
        rim_before = lax.dynamic_index_in_dim(rim_force, return_row[far_end], 0, keepdims=False)
        rim_force = lax.dynamic_update_index_in_dim(
            rim_force, rim_before + on_far, return_row[far_end], 0
        )
        return (slot_force, rim_force)

    start_slots = jnp.zeros((total_slots + 1, 3, points), jnp.float32)
    start_rims = jnp.zeros((2 * RIM_VES + 1, 3, points), jnp.float32)
    slot_force, rim_force = lax.fori_loop(0, live_pairs, add_pair, (start_slots, start_rims))
    from_rims = extended(rim_force[: 2 * RIM_VES], (("group", 0),), RIM_VES)
    rim_total = from_rims[:RIM_VES] + from_rims[3 * RIM_VES :]
    selector = (asked_for[None, :] == jnp.arange(vesicle_count)[:, None]).astype(jnp.float32)
    returned = lax.all_to_all(
        slot_force[:total_slots].reshape(members, slot_cap, 3, points),
        "member",
        split_axis=0,
        concat_axis=0,
        tiled=True,
    )
    point_total = jnp.dot(
        selector,
        returned.reshape(total_slots, 3 * points),
        precision=lax.Precision.HIGHEST,
        preferred_element_type=jnp.float32,
    )
    point_total = point_total.reshape(vesicle_count, 3, points).at[:RIM_VES].add(rim_total)
    return project(point_total, harmonics, weights)


def solution(mesh):
    return jax.shard_map(
        per_device,
        mesh=mesh,
        in_specs=(
            P(("group", "member"), None, None),
            P(("group", "member"), None),
            P(("group", "member"), None),
        ),
        out_specs=P(("group", "member"), None, None),
        check_vma=False,
    )
```

profile of v0, /device:TPU:8, one launch (start us, length us, event | category | flops | bytes accessed | tf_op | source)
XLA Modules:
  0.0 952.8 jit_solution(4044911006099247076)
XLA Ops:
  6.2 12.9 %all-to-all-start = ((s32[64,1,2]{2,1,0:T(1,128)}), s32[64,1,2]{2,1,0:T(1,128)S(1)}, u32[]{:S(2)}, u32[]{:S(2)}) async-start(s32[64,1,2]{2,1,0:T(1,128)} %bitcast.13), calls=%async_computation | async-start | bytes 65536 | tf_op jit(solution)/shard_map/all_to_all | solution.py:160
  169.8 28.4 %concatenate.75 = f32[256,2112]{1,0:T(8,128)S(1)} concatenate(f32[1,2112]{1,0:T(1,128)S(1)} %stack_reshape.34, f32[1,2112]{1,0:T(1,128)S(1)} %mul.36912, f32[1,2112]{1,0:T(1,128)S(1)} %stack_reshape.35, f32[1,2112]{1,0:T(1,128)S(1)} %mul.36919, f32[1,2112]{1,0:T(1,128)} %mul.36929, f32[1,2112]{1,0:T(1,128)S(1)} %mul.36935, f32[1,2112]{1,0:T(1,128)S(1)} %stack_reshape.36, ...), dimensions={0} | concatenate | bytes 4325376
  201.8 5.0 gather_fusion
  206.8 6.4 copy_select_fusion
  213.2 19.4 %all-to-all-start.1 = ((f32[64,2,3,2112]{3,1,2,0:T(2,128)}), f32[64,2,3,2112]{3,1,2,0:T(2,128)}, u32[]{:S(2)}, u32[]{:S(2)}) async-start(f32[64,2,3,2112]{3,1,2,0:T(2,128)} %copy_select_fusion), calls=%async_computation.1 | async-start | bytes 6684672 | tf_op jit(solution)/shard_map/all_to_all | solution.py:167
  234.0 3.0 collective-permute-start
  240.8 69.0 %all-to-all-done.1 = f32[64,2,3,2112]{3,1,2,0:T(2,128)} async-done(((f32[64,2,3,2112]{3,1,2,0:T(2,128)}), f32[64,2,3,2112]{3,1,2,0:T(2,128)}, u32[]{:S(2)}, u32[]{:S(2)}) %all-to-all-start.1) | async-done | bytes 3244064 | tf_op jit(solution)/shard_map/all_to_all | solution.py:167
  309.8 5.2 copy.90
  317.6 424.9 %while.15 = (s32[]{:T(128)}, f32[129,3,2112]{2,1,0:T(4,128)}, f32[9,3,2112]{2,0,1:T(8,128)S(1)}, s32[]{:T(128)}, s32[32]{0:T(128)S(1)}, /*index=5*/f32[128,3,211...) while((s32[]{:T(128)}, f32[129,3,2112]{2,1,0:T(4,128)}, ...), condition=%wide.region_29.30_spmd, body=%wide.region_4.29_spmd.sunk | while | flops 93760152 | bytes 1210773 | solution.py:208
  332.7 15.4 %fusion.86 = (f32[2112]{0:T(1024)S(1)}, f32[528]{0:T(1024)S(1)}, f32[2112]{0:T(1024)S(1)}, f32[2112]{0:T(1024)S(1)}, f32[528]{0:T(1024)S(1)}, /*index=5*/f32[528...) fusion(f32[528]{0:T(1024)S(1)} %get-tuple-element.869, ...), kind=kLoop, calls=%fused_computation.68.clone.1 | loop fusion | flops 93639744 | bytes 177408 | tf_op jit(solution)/shard_map/while/body/reduce_sum | solution.py:128
  365.4 15.4 %fusion.86 = (f32[2112]{0:T(1024)S(1)}, f32[528]{0:T(1024)S(1)}, f32[2112]{0:T(1024)S(1)}, f32[2112]{0:T(1024)S(1)}, f32[528]{0:T(1024)S(1)}, /*index=5*/f32[528...) fusion(f32[528]{0:T(1024)S(1)} %get-tuple-element.869, ...), kind=kLoop, calls=%fused_computation.68.clone.1 | loop fusion | flops 93639744 | bytes 177408 | tf_op jit(solution)/shard_map/while/body/reduce_sum | solution.py:128
  398.1 15.4 %fusion.86 = (f32[2112]{0:T(1024)S(1)}, f32[528]{0:T(1024)S(1)}, f32[2112]{0:T(1024)S(1)}, f32[2112]{0:T(1024)S(1)}, f32[528]{0:T(1024)S(1)}, /*index=5*/f32[528...) fusion(f32[528]{0:T(1024)S(1)} %get-tuple-element.869, ...), kind=kLoop, calls=%fused_computation.68.clone.1 | loop fusion | flops 93639744 | bytes 177408 | tf_op jit(solution)/shard_map/while/body/reduce_sum | solution.py:128
  430.8 15.4 %fusion.86 = (f32[2112]{0:T(1024)S(1)}, f32[528]{0:T(1024)S(1)}, f32[2112]{0:T(1024)S(1)}, f32[2112]{0:T(1024)S(1)}, f32[528]{0:T(1024)S(1)}, /*index=5*/f32[528...) fusion(f32[528]{0:T(1024)S(1)} %get-tuple-element.869, ...), kind=kLoop, calls=%fused_computation.68.clone.1 | loop fusion | flops 93639744 | bytes 177408 | tf_op jit(solution)/shard_map/while/body/reduce_sum | solution.py:128
  463.4 15.4 %fusion.86 = (f32[2112]{0:T(1024)S(1)}, f32[528]{0:T(1024)S(1)}, f32[2112]{0:T(1024)S(1)}, f32[2112]{0:T(1024)S(1)}, f32[528]{0:T(1024)S(1)}, /*index=5*/f32[528...) fusion(f32[528]{0:T(1024)S(1)} %get-tuple-element.869, ...), kind=kLoop, calls=%fused_computation.68.clone.1 | loop fusion | flops 93639744 | bytes 177408 | tf_op jit(solution)/shard_map/while/body/reduce_sum | solution.py:128
  496.1 15.4 %fusion.86 = (f32[2112]{0:T(1024)S(1)}, f32[528]{0:T(1024)S(1)}, f32[2112]{0:T(1024)S(1)}, f32[2112]{0:T(1024)S(1)}, f32[528]{0:T(1024)S(1)}, /*index=5*/f32[528...) fusion(f32[528]{0:T(1024)S(1)} %get-tuple-element.869, ...), kind=kLoop, calls=%fused_computation.68.clone.1 | loop fusion | flops 93639744 | bytes 177408 | tf_op jit(solution)/shard_map/while/body/reduce_sum | solution.py:128
  528.8 15.4 %fusion.86 = (f32[2112]{0:T(1024)S(1)}, f32[528]{0:T(1024)S(1)}, f32[2112]{0:T(1024)S(1)}, f32[2112]{0:T(1024)S(1)}, f32[528]{0:T(1024)S(1)}, /*index=5*/f32[528...) fusion(f32[528]{0:T(1024)S(1)} %get-tuple-element.869, ...), kind=kLoop, calls=%fused_computation.68.clone.1 | loop fusion | flops 93639744 | bytes 177408 | tf_op jit(solution)/shard_map/while/body/reduce_sum | solution.py:128
  561.4 15.4 %fusion.86 = (f32[2112]{0:T(1024)S(1)}, f32[528]{0:T(1024)S(1)}, f32[2112]{0:T(1024)S(1)}, f32[2112]{0:T(1024)S(1)}, f32[528]{0:T(1024)S(1)}, /*index=5*/f32[528...) fusion(f32[528]{0:T(1024)S(1)} %get-tuple-element.869, ...), kind=kLoop, calls=%fused_computation.68.clone.1 | loop fusion | flops 93639744 | bytes 177408 | tf_op jit(solution)/shard_map/while/body/reduce_sum | solution.py:128
  594.1 15.4 %fusion.86 = (f32[2112]{0:T(1024)S(1)}, f32[528]{0:T(1024)S(1)}, f32[2112]{0:T(1024)S(1)}, f32[2112]{0:T(1024)S(1)}, f32[528]{0:T(1024)S(1)}, /*index=5*/f32[528...) fusion(f32[528]{0:T(1024)S(1)} %get-tuple-element.869, ...), kind=kLoop, calls=%fused_computation.68.clone.1 | loop fusion | flops 93639744 | bytes 177408 | tf_op jit(solution)/shard_map/while/body/reduce_sum | solution.py:128
  626.8 15.4 %fusion.86 = (f32[2112]{0:T(1024)S(1)}, f32[528]{0:T(1024)S(1)}, f32[2112]{0:T(1024)S(1)}, f32[2112]{0:T(1024)S(1)}, f32[528]{0:T(1024)S(1)}, /*index=5*/f32[528...) fusion(f32[528]{0:T(1024)S(1)} %get-tuple-element.869, ...), kind=kLoop, calls=%fused_computation.68.clone.1 | loop fusion | flops 93639744 | bytes 177408 | tf_op jit(solution)/shard_map/while/body/reduce_sum | solution.py:128
  659.4 15.4 %fusion.86 = (f32[2112]{0:T(1024)S(1)}, f32[528]{0:T(1024)S(1)}, f32[2112]{0:T(1024)S(1)}, f32[2112]{0:T(1024)S(1)}, f32[528]{0:T(1024)S(1)}, /*index=5*/f32[528...) fusion(f32[528]{0:T(1024)S(1)} %get-tuple-element.869, ...), kind=kLoop, calls=%fused_computation.68.clone.1 | loop fusion | flops 93639744 | bytes 177408 | tf_op jit(solution)/shard_map/while/body/reduce_sum | solution.py:128
  692.1 15.4 %fusion.86 = (f32[2112]{0:T(1024)S(1)}, f32[528]{0:T(1024)S(1)}, f32[2112]{0:T(1024)S(1)}, f32[2112]{0:T(1024)S(1)}, f32[528]{0:T(1024)S(1)}, /*index=5*/f32[528...) fusion(f32[528]{0:T(1024)S(1)} %get-tuple-element.869, ...), kind=kLoop, calls=%fused_computation.68.clone.1 | loop fusion | flops 93639744 | bytes 177408 | tf_op jit(solution)/shard_map/while/body/reduce_sum | solution.py:128
  724.8 15.4 %fusion.86 = (f32[2112]{0:T(1024)S(1)}, f32[528]{0:T(1024)S(1)}, f32[2112]{0:T(1024)S(1)}, f32[2112]{0:T(1024)S(1)}, f32[528]{0:T(1024)S(1)}, /*index=5*/f32[528...) fusion(f32[528]{0:T(1024)S(1)} %get-tuple-element.869, ...), kind=kLoop, calls=%fused_computation.68.clone.1 | loop fusion | flops 93639744 | bytes 177408 | tf_op jit(solution)/shard_map/while/body/reduce_sum | solution.py:128
  742.6 3.0 slice.166
  745.6 3.4 copy.85
  749.0 105.1 %all-to-all-start.2 = ((f32[64,2,3,2112]{3,1,2,0:T(2,128)}), f32[64,2,3,2112]{3,1,2,0:T(2,128)}, u32[]{:S(2)}, u32[]{:S(2)}) async-start(f32[64,2,3,2112]{3,1,2,0:T(2,128)} %copy.85), calls=%async_computation.2 | async-start | bytes 6684672 | tf_op jit(solution)/shard_map/all_to_all | solution.py:212
  855.8 3.0 collective-permute-start.2
  858.8 71.0 %all-to-all-done.2 = f32[64,2,3,2112]{3,1,2,0:T(2,128)} async-done(((f32[64,2,3,2112]{3,1,2,0:T(2,128)}), f32[64,2,3,2112]{3,1,2,0:T(2,128)}, u32[]{:S(2)}, u32[]{:S(2)}) %all-to-all-start.2) | async-done | bytes 3244064 | tf_op jit(solution)/shard_map/all_to_all | solution.py:212
  929.8 5.1 copy.86
  934.9 6.2 reshape.7607
  941.1 4.9 copy.87
  946.0 3.5 fusion.61
  949.6 2.8 fusion.53
  (1040 shorter events, 258.9 us)
Async XLA Ops:
  4.4 24.5 %copy-start = (s32[32]{0:T(128)}, s32[32]{0:T(128)S(1)}, u32[]{:S(2)}) copy-start(s32[32]{0:T(128)S(1)} %get-tuple-element.592) | copy-start | bytes 388
  4.7 21.6 %copy-start.2 = (s32[32]{0:T(128)}, s32[32]{0:T(128)S(1)}, u32[]{:S(2)}) copy-start(s32[32]{0:T(128)S(1)} %select_reduce_fusion) | copy-start | bytes 388
  6.2 193.8 %all-to-all-start = ((s32[64,1,2]{2,1,0:T(1,128)}), s32[64,1,2]{2,1,0:T(1,128)S(1)}, u32[]{:S(2)}, u32[]{:S(2)}) async-start(s32[64,1,2]{2,1,0:T(1,128)} %bitcast.13), calls=%async_computation | async-start | bytes 65536 | tf_op jit(solution)/shard_map/all_to_all | solution.py:160
  213.2 23.9 %copy-start.1 = (s32[32]{0:T(128)S(1)}, s32[32]{0:T(128)}, u32[]{:S(2)}) copy-start(s32[32]{0:T(128)} %copy-done) | copy-start | bytes 388
  213.2 23.9 %copy-start.3 = (s32[32]{0:T(128)S(1)}, s32[32]{0:T(128)}, u32[]{:S(2)}) copy-start(s32[32]{0:T(128)} %copy-done.2) | copy-start | bytes 388
  213.2 26.6 %copy-start.4 = (f32[16,3]{0,1:T(4,128)S(1)}, f32[16,3]{0,1:T(4,128)}, u32[]{:S(2)}) copy-start(f32[16,3]{0,1:T(4,128)} %param.9) | copy-start | bytes 580
  213.2 96.5 %all-to-all-start.1 = ((f32[64,2,3,2112]{3,1,2,0:T(2,128)}), f32[64,2,3,2112]{3,1,2,0:T(2,128)}, u32[]{:S(2)}, u32[]{:S(2)}) async-start(f32[64,2,3,2112]{3,1,2,0:T(2,128)} %copy_select_fusion), calls=%async_computation.1 | async-start | bytes 6684672 | tf_op jit(solution)/shard_map/all_to_all | solution.py:167
  232.7 7.2 collective-permute-start.1
  234.0 5.9 collective-permute-start
  240.8 76.8 %copy-start.5 = (s32[32]{0:T(128)S(1)}, s32[32]{0:T(128)}, u32[]{:S(2)}) copy-start(s32[32]{0:T(128)} %get-tuple-element.925) | copy-start | bytes 388
  240.8 76.8 %copy-start.6 = (s32[32]{0:T(128)S(1)}, s32[32]{0:T(128)}, u32[]{:S(2)}) copy-start(s32[32]{0:T(128)} %get-tuple-element.923) | copy-start | bytes 388
  749.0 180.8 %all-to-all-start.2 = ((f32[64,2,3,2112]{3,1,2,0:T(2,128)}), f32[64,2,3,2112]{3,1,2,0:T(2,128)}, u32[]{:S(2)}, u32[]{:S(2)}) async-start(f32[64,2,3,2112]{3,1,2,0:T(2,128)} %copy.85), calls=%async_computation.2 | async-start | bytes 6684672 | tf_op jit(solution)/shard_map/all_to_all | solution.py:212
  854.5 95.1 %collective-permute-start.3 = (f32[4,3,2112]{2,0,1:T(4,128)S(1)}, f32[4,3,2112]{2,0,1:T(4,128)S(1)}, u32[]{:S(2)}, u32[]{:S(2)}) collective-permute-start(f32[4,3,2112]{2,0,1:T(4,128)S(1)} %get-tuple-element.312), channel_id=1, source_target_pairs={{64,0},{128,64},{192,128},{65,1},{129,65},{193,129},{66,2},{130,66... | collective-permute-start | bytes 304136 | tf_op jit(solution)/shard_map/ppermute | solution.py:21
  855.8 93.8 %collective-permute-start.2 = (f32[4,3,2112]{2,0,1:T(4,128)S(1)}, f32[4,3,2112]{2,0,1:T(4,128)S(1)}, u32[]{:S(2)}, u32[]{:S(2)}) collective-permute-start(f32[4,3,2112]{2,0,1:T(4,128)S(1)} %get-tuple-element.313), channel_id=1, source_target_pairs={{0,64},{64,128},{128,192},{1,65},{65,129},{129,193},{2,66},{66,130... | collective-permute-start | bytes 304136 | tf_op jit(solution)/shard_map/ppermute | solution.py:18
where the time goes:
time: 969 us; the launch traced here: 953 us
  local copies, waits for them, and re-layouts  262 us (27%)
  other arithmetic  261 us (27%)
  starting transfers between devices  146 us (15%)
  waiting for transfers between devices  140 us (14%)
  loops' own time  132 us (14%)
    reduce_sum x13, other arithmetic, pair_forces(): jnp.sum(kernel * delta_x, axis=0)  200 us
    mul x288, local copies, waits for them, and re-layouts, basis_table(): legendre[degree, abs(azimuth)][:, None] * beside_all[None, :]  139 us
    another operation x1, loops' own time, per_device(): lax.fori_loop(0, live_pairs, add_pair, (start_slots, start_rims))  132 us
    all_to_all x1, starting transfers between devices, per_device(): lax.all_to_all(slot_force[:total_slots].reshape(members, slot_cap, 3, poi...  105 us
    all_to_all x1, waiting for transfers between devices, per_device(): lax.all_to_all(slot_force[:total_slots].reshape(members, slot_cap, 3, poi...  71 us
    all_to_all x1, waiting for transfers between devices, per_device(): lax.all_to_all(outgoing.reshape(members, slot_cap, 3, points), 'member',...  69 us
    unnamed x17, local copies, waits for them, and re-layouts  30 us
    all_to_all x1, starting transfers between devices, per_device(): lax.all_to_all(outgoing.reshape(members, slot_cap, 3, points), 'member',...  19.4 us
  transfers between devices with their start and end apart: 7, of which 2 were waited for; matrix products, arithmetic and copies ran while one was open for 21% of the time, Pallas kernels for 0%

commit v1 on v0

v1 whole, which is shorter than its diff:
```python
import functools
import math

import jax
import jax.numpy as jnp
import numpy as np
from jax import lax
from jax.experimental import pallas as pl
from jax.experimental.pallas import tpu as pltpu
from jax.sharding import PartitionSpec as P

ORDER = 16
UPORDER = 32
RIM_VES = 4
LATS = UPORDER + 1
LONS = 2 * UPORDER
POINTS = LATS * LONS
NCOEF = (ORDER + 1) ** 2
LANES = 128
TILES = -(-POINTS // LANES)
PADDED = TILES * LANES
WIDTH = (0.7 * math.pi / LATS) ** 2
SCALE = 1.0 / math.sqrt(WIDTH)
FACTOR = math.sqrt(WIDTH) / (POINTS * WIDTH * WIDTH)
FAR_AWAY = 1e15
F32 = jnp.float32
HIGHEST = lax.Precision.HIGHEST


def factor_tables():
    theta = (np.arange(LATS) + 0.5) * (math.pi / LATS)
    phi = np.arange(LONS) * (2.0 * math.pi / LONS)
    cosine, sine = np.cos(theta), np.sin(theta)
    legendre = {}
    diagonal = np.full_like(cosine, math.sqrt(1.0 / (4.0 * math.pi)))
    for m in range(ORDER + 1):
        if m > 0:
            diagonal = -math.sqrt((2.0 * m + 1.0) / (2.0 * m)) * sine * diagonal
        legendre[m, m] = diagonal
        if m < ORDER:
            legendre[m + 1, m] = math.sqrt(2.0 * m + 3.0) * cosine * diagonal
        for l in range(m + 2, ORDER + 1):
            one = math.sqrt((4.0 * l * l - 1.0) / (l * l - m * m))
            two = math.sqrt(((l - 1.0) ** 2 - m * m) / (4.0 * (l - 1.0) ** 2 - 1.0))
            legendre[l, m] = one * (cosine * legendre[l - 1, m] - two * legendre[l - 2, m])
    lat = np.zeros((3 * LANES, LANES))
    lon = np.zeros((3 * LANES, LANES))
    row = 0
    for l in range(ORDER + 1):
        for m in range(-l, l + 1):
            lat[row, :LATS] = legendre[l, abs(m)]
            if m == 0:
                wave = np.ones(LONS)
            elif m > 0:
                wave = math.sqrt(2.0) * np.cos(m * phi)
            else:
                wave = math.sqrt(2.0) * np.sin(-m * phi)
            lon[row, :LONS] = wave
            lon[row, LONS:] = wave
            row += 1
    weights = np.zeros((8, PADDED))
    weights[:, :POINTS] = np.repeat(sine * (math.pi / LATS) * (2.0 * math.pi / LONS), LONS) * FACTOR
    return lat.astype(np.float32), lon.astype(np.float32), weights.astype(np.float32)


def pick_kernel(asked_ref, tiles_ref, out_ref):
    def pick(slot, carry):
        source = jnp.maximum(asked_ref[slot], 0)
        out_ref[slot] = tiles_ref[source]
        return carry

    lax.fori_loop(0, out_ref.shape[0], pick, 0, unroll=8)


def pair_kernel(
    slots,
    rows,
    meta_ref,
    offset_ref,
    lat_ref,
    lon_ref,
    weight_ref,
    received_ref,
    low_ref,
    high_ref,
    slot_out,
    low_out,
    high_out,
    source,
    ends,
    basis,
    surface,
    turned,
    force,
    near_turned,
    far_wide,
    far_sum,
    near_wide,
    near_sum,
):
    pairs = meta_ref.shape[0] // 2
    sub = rows // 8
    blocks = POINTS // rows
    count = slots.total
    live = meta_ref[2 * pairs]
    rims = low_ref.shape[0] // 8

    source[: count * 8] = received_ref[...]
    source[count * 8 : (count + rims) * 8] = low_ref[...]
    source[(count + rims) * 8 :] = high_ref[...]
    for pair in range(pairs):
        for side in range(2):
            start = pl.multiple_of(meta_ref[side * pairs + pair] * 8, 8)
            ends[(side * pairs + pair) * 8 : (side * pairs + pair + 1) * 8] = source[pl.ds(start, 8)]

    def chunk(index):
        return ends[pl.ds(index, 2 * pairs, stride=8), :]

    tails = chunk(6)
    tail_rows = [tails, pltpu.roll(tails, LANES // 2, 1), chunk(7)]
    coefs = jnp.concatenate(
        [
            jnp.concatenate([chunk(2 * c), chunk(2 * c + 1), tail_rows[c]], axis=1)
            for c in range(3)
        ],
        axis=0,
    )
    shift = offset_ref[...] * SCALE
    lane = lax.broadcasted_iota(jnp.int32, (8, LANES), 1)
    half = lax.broadcasted_iota(jnp.int32, lat_ref.shape, 1) < LONS
    for t in range(TILES):
        lanes = slice(t * LANES, (t + 1) * LANES)
        lat = jnp.where(half, lat_ref[:, 2 * t : 2 * t + 1], lat_ref[:, 2 * t + 1 : 2 * t + 2])
        table = lat * lon_ref[...]
        basis[:, lanes] = table
        part = jnp.dot(coefs, table, precision=HIGHEST, preferred_element_type=F32)
        part = part * SCALE + shift
        if t == TILES - 1:
            valid = lax.broadcasted_iota(jnp.int32, part.shape, 1) < POINTS - t * LANES
            part = jnp.where(valid, part, FAR_AWAY)
        surface[:, lanes] = part
        near = jnp.concatenate(
            [part[c * 2 * pairs : c * 2 * pairs + pairs] for c in range(3)]
            + [jnp.zeros((LANES - 3 * pairs, LANES), F32)],
            axis=0,
        )
        turned[lanes, :] = near.T
    near_turned[...] = jnp.zeros_like(near_turned)
    force[...] = jnp.zeros_like(force)

    lane_wide = lax.broadcasted_iota(jnp.int32, (rows, LANES), 1)

    def spread(pair, block):
        start = pl.multiple_of(block * rows, 8)
        columns = pltpu.roll(turned[pl.ds(start, rows), :], lax.rem(LANES - pair, LANES), 1)
        for c in range(3):
            column = columns[:, c * pairs : c * pairs + 1]
            near_wide[c] = jnp.broadcast_to(column, (rows, LANES)).reshape(sub, 8, LANES)

    def gather_near(pair, block):
        start = pl.multiple_of(block * rows, 8)
        value = near_turned[pl.ds(start, rows), :]
        for c in range(3):
            total = jnp.sum(near_sum[c].reshape(rows, LANES), axis=1, keepdims=True)
            value = jnp.where(lane_wide == c * pairs + pair, total, value)
        near_turned[pl.ds(start, rows), :] = value

    def one_pair(pair, carry):
        for c in range(3):
            row = surface[pl.ds(c * 2 * pairs + pairs + pair, 1), :]
            far_wide[c] = jnp.broadcast_to(row, (8, PADDED))
        far_sum[...] = jnp.zeros_like(far_sum)
        near_sum[...] = jnp.zeros_like(near_sum)
        spread(pair, 0)

        def one_block(block, inner):
            near = [near_wide[c] for c in range(3)]
            gather_near(pair, jnp.maximum(block - 1, 0))
            spread(pair, jnp.minimum(block + 1, blocks - 1))
            near_acc = [jnp.zeros((sub, 8, LANES), F32) for _ in range(3)]
            for t in range(TILES):
                lanes = slice(t * LANES, (t + 1) * LANES)
                delta = [near[c] - far_wide[c, :, lanes][None] for c in range(3)]
                grown = (delta[0] * delta[0] + delta[1] * delta[1]) + (delta[2] * delta[2] + 1.0)
                kernel = 1.0 / grown
                kernel = kernel * kernel
                for c in range(3):
                    pull = kernel * delta[c]
                    near_acc[c] = near_acc[c] + pull
                    far_sum[c, :, lanes] = far_sum[c, :, lanes] + jnp.sum(pull, axis=0)
            for c in range(3):
                near_sum[c] = near_acc[c]
            return inner

        lax.fori_loop(0, blocks, one_block, 0)
        gather_near(pair, blocks - 1)
        for c in range(3):
            force[pl.ds(c * 2 * pairs + pairs + pair, 1), :] = -jnp.sum(
                far_sum[c], axis=0, keepdims=True
            )
        return carry

    lax.fori_loop(0, live, one_pair, 0)

    total = jnp.zeros((6 * pairs, 3 * LANES), F32)
    for t in range(TILES):
        lanes = slice(t * LANES, (t + 1) * LANES)
        near = near_turned[lanes, :].T
        for c in range(3):
            force[c * 2 * pairs : c * 2 * pairs + pairs, lanes] = near[c * pairs : (c + 1) * pairs]
        part = force[:, lanes] * weight_ref[0:1, lanes]
        total = total + lax.dot_general(
            part,
            basis[:, lanes],
            (((1,), (1,)), ((), ())),
            precision=HIGHEST,
            preferred_element_type=F32,
        )
    for c in range(3):
        block = total[c * 2 * pairs : (c + 1) * 2 * pairs]
        ends[pl.ds(2 * c, 2 * pairs, stride=8), :] = block[:, :LANES]
        ends[pl.ds(2 * c + 1, 2 * pairs, stride=8), :] = block[:, LANES : 2 * LANES]
    tail = [total[c * 2 * pairs : (c + 1) * 2 * pairs, 2 * LANES :] for c in range(3)]
    ends[pl.ds(6, 2 * pairs, stride=8), :] = tail[0] + pltpu.roll(tail[1], LANES // 2, 1)
    ends[pl.ds(7, 2 * pairs, stride=8), :] = tail[2]

    source[...] = jnp.zeros_like(source)

    def hand_out(pair, carry):
        for side in range(2):
            value = ends[pl.ds(pl.multiple_of((side * pairs + pair) * 8, 8), 8), :]
            start = pl.multiple_of(meta_ref[side * pairs + pair] * 8, 8)
            source[pl.ds(start, 8), :] = source[pl.ds(start, 8), :] + value
        return carry

    lax.fori_loop(0, live, hand_out, 0)
    slot_out[...] = source[: count * 8]
    low_out[...] = source[count * 8 : (count + rims) * 8]
    high_out[...] = source[(count + rims) * 8 :]


def collect_kernel(asked_ref, returned_ref, low_ref, high_ref, out_ref, total):
    vesicles = out_ref.shape[0]
    total[...] = jnp.zeros_like(total)
    rims = low_ref.shape[0]
    total[:rims] = low_ref[...] + high_ref[...]

    def add(slot, carry):
        asked = asked_ref[slot]
        row = jnp.where(asked >= 0, asked, vesicles)
        total[row] = total[row] + returned_ref[slot]
        return carry

    lax.fori_loop(0, returned_ref.shape[0], add, 0, unroll=4)
    rest = NCOEF - 2 * LANES
    for v in range(vesicles):
        for c in range(3):
            out_ref[v, c : c + 1, :LANES] = total[v, 2 * c : 2 * c + 1, :]
            out_ref[v, c : c + 1, LANES : 2 * LANES] = total[v, 2 * c + 1 : 2 * c + 2, :]
        out_ref[v, 0:1, 2 * LANES :] = total[v, 6:7, :rest]
        moved = pltpu.roll(total[v], LANES // 2, 1)
        out_ref[v, 1:2, 2 * LANES :] = moved[6:7, :rest]
        out_ref[v, 2:3, 2 * LANES :] = total[v, 7:8, :rest]


class Slots:
    def __init__(self, members, cap):
        self.members = members
        self.cap = cap
        self.total = members * cap

    def __repr__(self):
        return "slots"


def vmem():
    return pl.BlockSpec(memory_space=pltpu.VMEM)


def smem():
    return pl.BlockSpec(memory_space=pltpu.SMEM)


def per_device(coefficients, pair_list, pair_offset):
    members = lax.axis_size("member")
    groups = lax.axis_size("group")
    group_here = lax.axis_index("group")
    vesicles = coefficients.shape[0]
    pairs = pair_list.shape[0]
    slots = Slots(members, max(2, (2 * pairs + members - 1) // members))
    total_slots = slots.total
    forward = [(i, i + 1) for i in range(groups - 1)]
    backward = [(i + 1, i) for i in range(groups - 1)]

    end_ids = pair_list.T.reshape(-1)
    end_live = end_ids >= 0
    safe_ids = jnp.maximum(end_ids, 0)
    owner_device = safe_ids // vesicles
    owner_group = owner_device // members
    owner_member = owner_device % members
    owner_slot = safe_ids % vesicles
    inside = end_live & (owner_group == group_here)
    key = jnp.where(inside, owner_member, -1)
    order = jnp.arange(2 * pairs)
    same = (key[:, None] == key[None, :]) & (order[None, :] < order[:, None])
    earlier = jnp.sum(same.astype(jnp.int32), axis=1)
    end_slot = jnp.where(inside, owner_member * slots.cap + earlier, -1)
    hit = end_slot[None, :] == jnp.arange(total_slots)[:, None]
    request = jnp.max(jnp.where(hit, owner_slot[None, :], -1), axis=1)
    asked_for = lax.all_to_all(
        request.reshape(members, slots.cap), "member", split_axis=0, concat_axis=0, tiled=True
    ).reshape(-1)

    head = coefficients[:, :, : 2 * LANES].reshape(vesicles, 6, LANES)
    tail = jnp.pad(coefficients[:, :, 2 * LANES :], ((0, 0), (0, 1), (0, LANES // 2 - (NCOEF - 2 * LANES))))
    tiles = jnp.concatenate([head, tail.reshape(vesicles, 2, LANES)], axis=1)
    rim = tiles[:RIM_VES]
    low = lax.ppermute(rim, "group", forward)
    high = lax.ppermute(rim, "group", backward)

    outgoing = pl.pallas_call(
        pick_kernel,
        out_shape=jax.ShapeDtypeStruct((total_slots, 8, LANES), F32),
        in_specs=[smem(), vmem()],
        out_specs=vmem(),
        name="pick",
    )(asked_for, tiles)
    received = lax.all_to_all(
        outgoing.reshape(members, slots.cap, 8, LANES),
        "member",
        split_axis=0,
        concat_axis=0,
        tiled=True,
    )

    rim_row = (
        total_slots
        + jnp.where(owner_group < group_here, 0, RIM_VES)
        + jnp.minimum(owner_slot, RIM_VES - 1)
    )
    end_row = jnp.where(inside, end_slot, jnp.where(end_live, rim_row, 0))
    live_pairs = jnp.sum((pair_list[:, 0] >= 0).astype(jnp.int32))
    meta = jnp.concatenate([end_row, live_pairs[None]]).astype(jnp.int32)
    offsets = jnp.pad(pair_offset.T, ((0, 0), (0, pairs))).reshape(-1, 1)

    lat, lon, weights = factor_tables()
    rows = 96
    slot_force, low_force, high_force = pl.pallas_call(
        functools.partial(pair_kernel, slots, rows),
        out_shape=(
            jax.ShapeDtypeStruct((total_slots * 8, LANES), F32),
            jax.ShapeDtypeStruct((RIM_VES * 8, LANES), F32),
            jax.ShapeDtypeStruct((RIM_VES * 8, LANES), F32),
        ),
        in_specs=[smem()] + [vmem()] * 7,
        out_specs=(vmem(),) * 3,
        scratch_shapes=[
            pltpu.VMEM(((total_slots + 2 * RIM_VES) * 8, LANES), F32),
            pltpu.VMEM((2 * pairs * 8, LANES), F32),
            pltpu.VMEM((3 * LANES, PADDED), F32),
            pltpu.VMEM((6 * pairs, PADDED), F32),
            pltpu.VMEM((PADDED, LANES), F32),
            pltpu.VMEM((6 * pairs, PADDED), F32),
            pltpu.VMEM((PADDED, LANES), F32),
            pltpu.VMEM((3, 8, PADDED), F32),
            pltpu.VMEM((3, 8, PADDED), F32),
            pltpu.VMEM((3, rows // 8, 8, LANES), F32),
            pltpu.VMEM((3, rows // 8, 8, LANES), F32),
        ],
        compiler_params=pltpu.CompilerParams(vmem_limit_bytes=48 << 20),
        name="pair_forces",
    )(
        meta,
        offsets,
        jnp.asarray(lat),
        jnp.asarray(lon),
        jnp.asarray(weights),
        received.reshape(total_slots * 8, LANES),
        low.reshape(RIM_VES * 8, LANES),
        high.reshape(RIM_VES * 8, LANES),
    )
    returned = lax.all_to_all(
        slot_force.reshape(members, slots.cap, 8, LANES),
        "member",
        split_axis=0,
        concat_axis=0,
        tiled=True,
    )
    from_low = lax.ppermute(high_force.reshape(RIM_VES, 8, LANES), "group", forward)
    from_high = lax.ppermute(low_force.reshape(RIM_VES, 8, LANES), "group", backward)
    return pl.pallas_call(
        collect_kernel,
        out_shape=jax.ShapeDtypeStruct(coefficients.shape, F32),
        in_specs=[smem()] + [vmem()] * 3,
        out_specs=vmem(),
        scratch_shapes=[pltpu.VMEM((vesicles + 1, 8, LANES), F32)],
        name="collect",
    )(asked_for, returned.reshape(total_slots, 8, LANES), from_low, from_high)


def solution(mesh):
    return jax.shard_map(
        per_device,
        mesh=mesh,
        in_specs=(
            P(("group", "member"), None, None),
            P(("group", "member"), None),
            P(("group", "member"), None),
        ),
        out_specs=P(("group", "member"), None, None),
        check_vma=False,
    )
```

time: 969 us -> 336 us (0.35); the launches traced: 953 us -> 335 us
  other arithmetic: 261 us -> 3.01 us
  local copies, waits for them, and re-layouts: 262 us -> 6.76 us
  Pallas kernels: 0 us -> 216 us
  loops' own time: 132 us -> 0 us
  waiting for transfers between devices: 140 us -> 32.3 us
  starting transfers between devices: 146 us -> 77.5 us
    pallas_call x0 -> x3, Pallas kernels: none -> 216 us  [the longest x1 211 us: per_device(): pl.pallas_call(functools.partial(pair_kernel, slots, rows), out_shape=(ja...]
    reduce_sum x14 -> x2, other arithmetic: 200 us -> 0.81 us  [the longest x1 0.63 us: per_device(): live_pairs = jnp.sum((pair_list[:, 0] >= 0).astype(jnp.int32))]
    mul x290 -> x0, local copies, waits for them, and re-layouts: 139 us -> none  [the longest x288 139 us: basis_table(): legendre[degree, abs(azimuth)][:, None] * beside_all[None, :]]
    another operation x1 -> x0, loops' own time: 132 us -> none  [per_device(): lax.fori_loop(0, live_pairs, add_pair, (start_slots, start_rims))]
    all_to_all x3, waiting for transfers between devices: 140 us -> 27.7 us  [the longest x1 10.9 us: per_device(): lax.all_to_all(outgoing.reshape(members, slots.cap, 8, LANES), 'member',...]
    all_to_all x3, starting transfers between devices: 137 us -> 70.6 us  [the longest x1 52.1 us: per_device(): lax.all_to_all(slot_force.reshape(members, slots.cap, 8, LANES), 'member'...]
    dynamic_slice x65 -> x0, local copies, waits for them, and re-layouts: 34.5 us -> none  [the longest x13 8.62 us: add_pair(): far_slot = jnp.minimum(end_slot[far_end], total_slots - 1)]
    unnamed x17, local copies, waits for them, and re-layouts: 30 us -> 1.49 us
  transfers between devices with their start and end apart: 7 -> 7, of which waited for: 2 -> 4; matrix products, arithmetic and copies ran while one was open for 21% -> 1% of each run, Pallas kernels for 0% -> 0%
where the time goes in v1:
time: 336 us; the launch traced here: 335 us
  Pallas kernels  216 us (64%)
  starting transfers between devices  77.5 us (23%)
  waiting for transfers between devices  32.3 us (10%)
  local copies, waits for them, and re-layouts  6.76 us (2%)
    pallas_call x1, Pallas kernels, per_device(): pl.pallas_call(functools.partial(pair_kernel, slots, rows), out_shape=(ja...  211 us
    all_to_all x1, starting transfers between devices, per_device(): lax.all_to_all(slot_force.reshape(members, slots.cap, 8, LANES), 'member'...  52.1 us
    all_to_all x1, starting transfers between devices, per_device(): lax.all_to_all(request.reshape(members, slots.cap), 'member', split_axis=...  12.9 us
    all_to_all x1, waiting for transfers between devices, per_device(): lax.all_to_all(outgoing.reshape(members, slots.cap, 8, LANES), 'member',...  10.9 us
    all_to_all x1, waiting for transfers between devices, per_device(): lax.all_to_all(slot_force.reshape(members, slots.cap, 8, LANES), 'member'...  9.37 us
    all_to_all x1, waiting for transfers between devices, per_device(): lax.all_to_all(request.reshape(members, slots.cap), 'member', split_axis=...  7.37 us
  transfers between devices with their start and end apart: 7, of which 4 were waited for; matrix products, arithmetic and copies ran while one was open for 1% of the time, Pallas kernels for 0%

profile of v1, /device:TPU:8, one launch (start us, length us, event | category | flops | bytes accessed | tf_op | source)
XLA Modules:
  0.0 335.3 jit_solution(5838024051681418846)
XLA Ops:
  0.0 0.7 copy-done.6
  0.7 0.1 ne.116
  0.8 0.1 ge.26
  1.1 0.2 convert_reduce_fusion
  1.3 0.1 select_reduce_fusion
  1.3 0.8 all_to_all.12
  2.1 12.9 %all-to-all-start = ((s32[64,1,2]{2,1,0:T(1,128)}), s32[64,1,2]{2,1,0:T(1,128)S(1)}, u32[]{:S(2)}, u32[]{:S(2)}) async-start(s32[64,1,2]{2,1,0:T(1,128)} %bitcast.4), calls=%async_computation | async-start | bytes 65536 | tf_op jit(solution)/shard_map/all_to_all | solution.py:310
  15.1 0.7 slice-done
  15.8 0.1 reshape.170
  15.9 0.6 slice-done.1
  16.5 0.6 pad_maximum_fusion.tiles_ref
  17.2 7.4 %all-to-all-done = s32[64,1,2]{2,1,0:T(1,128)S(1)} async-done(((s32[64,1,2]{2,1,0:T(1,128)}), s32[64,1,2]{2,1,0:T(1,128)S(1)}, u32[]{:S(2)}, u32[]{:S(2)}) %all-to-all-start) | async-done | bytes 544 | tf_op jit(solution)/shard_map/all_to_all | solution.py:310
  24.5 0.5 broadcast.344
  25.0 0.7 reduce.4
  25.8 0.7 reshape.167.asked_ref
  26.4 1.8 pick.1
  28.3 5.6 %all-to-all-start.1 = ((f32[64,2,8,128]{3,2,1,0:T(8,128)}), f32[64,2,8,128]{3,2,1,0:T(8,128)S(1)}, u32[]{:S(2)}, u32[]{:S(2)}) async-start(f32[64,2,8,128]{3,2,1,0:T(8,128)} %bitcast.24), calls=%async_computation.1 | async-start | bytes 1048576 | tf_op jit(solution)/shard_map/all_to_all | solution.py:328
  33.9 1.3 collective-permute-start.1
  35.2 3.0 collective-permute-start
  38.2 0.6 fusion.6
  38.9 0.7 pad_add_fusion.meta_ref
  39.6 0.1 reshape.179.offset_ref
  39.7 10.9 %all-to-all-done.1 = f32[64,2,8,128]{3,2,1,0:T(8,128)S(1)} async-done(((f32[64,2,8,128]{3,2,1,0:T(8,128)}), f32[64,2,8,128]{3,2,1,0:T(8,128)S(1)}, u32[]{:S(2)}, u32[]{:S(2)}) %all-to-all-start.1) | async-done | bytes 524320 | tf_op jit(solution)/shard_map/all_to_all | solution.py:328
  50.7 211.3 %pair_forces.1 = (f32[1024,128]{1,0:T(8,128)}, f32[32,128]{1,0:T(8,128)S(1)}, f32[32,128]{1,0:T(8,128)S(1)}) custom-call(s32[33]{0:T(128)S(1)} %pad_add_fusion.meta_ref, f32[96,1]{1,0:T(8,128)S(1)} %reshape.179.offset_ref, f32[384,128]{1,0:T(8,128)S(1)} %copy-done.1, f32[384,128]{1,0:T(8,128)S(1)} %copy-done, f32[8,2176]{1,0:T(8,128)S(1)} %copy-done.2, ...), custom_call_target="tpu_custom_call" | custom-call | tf_op jit(solution)/shard_map/pair_forces/pallas_call | solution.py:348
  262.0 52.1 %all-to-all-start.2 = ((f32[64,2,8,128]{3,2,1,0:T(8,128)}), f32[64,2,8,128]{3,2,1,0:T(8,128)S(1)}, u32[]{:S(2)}, u32[]{:S(2)}) async-start(f32[64,2,8,128]{3,2,1,0:T(8,128)} %bitcast.11), calls=%async_computation.2 | async-start | bytes 1048576 | tf_op jit(solution)/shard_map/all_to_all | solution.py:382
  314.1 1.3 collective-permute-start.2
  315.4 1.3 collective-permute-start.3
  316.7 4.6 %collective-permute-done.3.high_ref = f32[4,8,128]{2,1,0:T(8,128)S(1)} collective-permute-done((f32[4,8,128]{2,1,0:T(8,128)S(1)}, f32[4,8,128]{2,1,0:T(8,128)S(1)}, u32[]{:S(2)}, u32[]{:S(2)}) %collective-permute-start.3) | collective-permute-done | bytes 16416 | tf_op jit(solution)/shard_map/ppermute | solution.py:390
  321.3 9.4 %all-to-all-done.2 = f32[64,2,8,128]{3,2,1,0:T(8,128)S(1)} async-done(((f32[64,2,8,128]{3,2,1,0:T(8,128)}), f32[64,2,8,128]{3,2,1,0:T(8,128)S(1)}, u32[]{:S(2)}, u32[]{:S(2)}) %all-to-all-start.2) | async-done | bytes 524320 | tf_op jit(solution)/shard_map/all_to_all | solution.py:382
  330.7 0.8 copy-done.3
  331.4 2.5 collect.1
  333.9 1.4 copy.24
  (31 shorter events, 0.3 us)
Async XLA Ops:
  0.0 0.7 copy-start.6
  2.1 22.4 %all-to-all-start = ((s32[64,1,2]{2,1,0:T(1,128)}), s32[64,1,2]{2,1,0:T(1,128)S(1)}, u32[]{:S(2)}, u32[]{:S(2)}) async-start(s32[64,1,2]{2,1,0:T(1,128)} %bitcast.4), calls=%async_computation | async-start | bytes 65536 | tf_op jit(solution)/shard_map/all_to_all | solution.py:310
  15.1 0.7 slice-start
  15.8 0.7 slice-start.1
  28.3 11.3 %copy-start.7 = (f32[16,3]{0,1:T(4,128)S(1)}, f32[16,3]{0,1:T(4,128)}, u32[]{:S(2)}) copy-start(f32[16,3]{0,1:T(4,128)} %param.8) | copy-start | bytes 580
  28.3 22.4 %copy-start = (f32[384,128]{1,0:T(8,128)S(1)}, f32[384,128]{1,0:T(8,128)}, u32[]{:S(2)}) copy-start(f32[384,128]{1,0:T(8,128)} %constant.92.clone.lon_ref) | copy-start | bytes 589828
  28.3 22.4 %copy-start.1 = (f32[384,128]{1,0:T(8,128)S(1)}, f32[384,128]{1,0:T(8,128)}, u32[]{:S(2)}) copy-start(f32[384,128]{1,0:T(8,128)} %constant.91.clone.lat_ref) | copy-start | bytes 589828
  28.3 22.4 %all-to-all-start.1 = ((f32[64,2,8,128]{3,2,1,0:T(8,128)}), f32[64,2,8,128]{3,2,1,0:T(8,128)S(1)}, u32[]{:S(2)}, u32[]{:S(2)}) async-start(f32[64,2,8,128]{3,2,1,0:T(8,128)} %bitcast.24), calls=%async_computation.1 | async-start | bytes 1048576 | tf_op jit(solution)/shard_map/all_to_all | solution.py:328
  33.8 16.8 %copy-start.2 = (f32[8,2176]{1,0:T(8,128)S(1)}, f32[8,2176]{1,0:T(8,128)}, u32[]{:S(2)}) copy-start(f32[8,2176]{1,0:T(8,128)} %constant.93.clone.weight_ref) | copy-start | bytes 208900
  33.9 5.8 %collective-permute-start.1 = (f32[4,8,128]{2,1,0:T(8,128)S(1)}, f32[4,8,128]{2,1,0:T(8,128)S(1)}, u32[]{:S(2)}, u32[]{:S(2)}) collective-permute-start(f32[4,8,128]{2,1,0:T(8,128)S(1)} %fusion), channel_id=1, source_target_pairs={{64,0},{128,64},{192,128},{65,1},{129,65},{193,129},{66,2},{130,66... | collective-permute-start | bytes 49160 | tf_op jit(solution)/shard_map/ppermute | solution.py:319
  35.2 4.5 %collective-permute-start = (f32[4,8,128]{2,1,0:T(8,128)S(1)}, f32[4,8,128]{2,1,0:T(8,128)S(1)}, u32[]{:S(2)}, u32[]{:S(2)}) collective-permute-start(f32[4,8,128]{2,1,0:T(8,128)S(1)} %fusion), channel_id=1, source_target_pairs={{0,64},{64,128},{128,192},{1,65},{65,129},{129,193},{2,66},{66,130... | collective-permute-start | bytes 49160 | tf_op jit(solution)/shard_map/ppermute | solution.py:318
  262.0 68.7 %all-to-all-start.2 = ((f32[64,2,8,128]{3,2,1,0:T(8,128)}), f32[64,2,8,128]{3,2,1,0:T(8,128)S(1)}, u32[]{:S(2)}, u32[]{:S(2)}) async-start(f32[64,2,8,128]{3,2,1,0:T(8,128)} %bitcast.11), calls=%async_computation.2 | async-start | bytes 1048576 | tf_op jit(solution)/shard_map/all_to_all | solution.py:382
  314.1 2.6 collective-permute-start.2
  315.4 5.9 %collective-permute-start.3 = (f32[4,8,128]{2,1,0:T(8,128)S(1)}, f32[4,8,128]{2,1,0:T(8,128)S(1)}, u32[]{:S(2)}, u32[]{:S(2)}) collective-permute-start(f32[4,8,128]{2,1,0:T(8,128)S(1)} %bitcast.22), channel_id=1, source_target_pairs={{64,0},{128,64},{192,128},{65,1},{129,65},{193,129},{66,2},{130,66... | collective-permute-start | bytes 49160 | tf_op jit(solution)/shard_map/ppermute | solution.py:390
  316.7 14.0 %copy-start.4 = (f32[4,8,128]{2,1,0:T(8,128)}, f32[4,8,128]{2,1,0:T(8,128)S(1)}, u32[]{:S(2)}) copy-start(f32[4,8,128]{2,1,0:T(8,128)S(1)} %collective-permute-done.2.low_ref) | copy-start | bytes 49156
  321.3 9.4 %copy-start.5 = (f32[4,8,128]{2,1,0:T(8,128)}, f32[4,8,128]{2,1,0:T(8,128)S(1)}, u32[]{:S(2)}) copy-start(f32[4,8,128]{2,1,0:T(8,128)S(1)} %collective-permute-done.3.high_ref) | copy-start | bytes 49156
  330.7 0.8 copy-start.3

commit v2 on v1

--- a/solution.py
+++ b/solution.py
@@ -22,8 +22,12 @@
 WIDTH = (0.7 * math.pi / LATS) ** 2
 SCALE = 1.0 / math.sqrt(WIDTH)
 FACTOR = math.sqrt(WIDTH) / (POINTS * WIDTH * WIDTH)
-FAR_AWAY = 1e15
+FAR_AWAY = 1e18
 F32 = jnp.float32
+BF16 = jnp.bfloat16
+FEATURES = 64
+SMALL = 16
+COORDS = 48
 HIGHEST = lax.Precision.HIGHEST
 
 
@@ -90,9 +94,12 @@
     ends,
     basis,
     surface,
-    turned,
     force,
     near_turned,
+    near_rows,
+    near_side,
+    far_rows,
+    far_side,
     far_wide,
     far_sum,
     near_wide,
@@ -125,9 +132,9 @@
         ],
         axis=0,
     )
-    shift = offset_ref[...] * SCALE
-    lane = lax.broadcasted_iota(jnp.int32, (8, LANES), 1)
+    shift = offset_ref[...] * (0.5 * SCALE)
     half = lax.broadcasted_iota(jnp.int32, lat_ref.shape, 1) < LONS
+    widest = jnp.zeros((6 * pairs, LANES), F32)
     for t in range(TILES):
         lanes = slice(t * LANES, (t + 1) * LANES)
         lat = jnp.where(half, lat_ref[:, 2 * t : 2 * t + 1], lat_ref[:, 2 * t + 1 : 2 * t + 2])
@@ -137,63 +144,158 @@
         part = part * SCALE + shift
         if t == TILES - 1:
             valid = lax.broadcasted_iota(jnp.int32, part.shape, 1) < POINTS - t * LANES
-            part = jnp.where(valid, part, FAR_AWAY)
+            part = jnp.where(valid, part, 0.0)
         surface[:, lanes] = part
-        near = jnp.concatenate(
-            [part[c * 2 * pairs : c * 2 * pairs + pairs] for c in range(3)]
-            + [jnp.zeros((LANES - 3 * pairs, LANES), F32)],
-            axis=0,
-        )
-        turned[lanes, :] = near.T
+        widest = jnp.maximum(widest, jnp.abs(part))
+    reach = jnp.max(widest, axis=1, keepdims=True)
+    reach = functools.reduce(
+        jnp.maximum, [reach[k * pairs : (k + 1) * pairs] for k in range(6)]
+    )
+    step = jnp.full_like(reach, 0.25)
+    for power in range(-2, 12):
+        step = jnp.where(reach > 256.0 * 2.0**power, 2.0 ** (power + 1), step)
+    inverse = jnp.full_like(reach, 4.0)
+    for power in range(-2, 12):
+        inverse = jnp.where(reach > 256.0 * 2.0**power, 2.0 ** -(power + 1), inverse)
+    square = step * step
+
+    def rounded(value):
+        return value.astype(BF16).astype(F32)
+
+    def in_pieces(value):
+        first = rounded(value)
+        second = rounded(value - first)
+        return [first, second, rounded(value - first - second)]
+
+    def on_grid(values):
+        whole = [jnp.round(v * inverse) for v in values]
+        rest = [v * inverse - w for v, w in zip(values, whole)]
+        upper = [rounded(r) for r in rest]
+        lower = [rounded(r - u) for r, u in zip(rest, upper)]
+        exact = whole[0] * whole[0] + whole[1] * whole[1] + whole[2] * whole[2]
+        small = [2.0 * w * r + r * r for w, r in zip(whole, rest)]
+        return whole, upper, lower, exact, small[0] + small[1] + small[2]
+
+    for t in range(TILES):
+        lanes = slice(t * LANES, (t + 1) * LANES)
+        near = [surface[c * 2 * pairs : c * 2 * pairs + pairs, lanes] for c in range(3)]
+        far = [surface[c * 2 * pairs + pairs : (c + 1) * 2 * pairs, lanes] for c in range(3)]
+        one = jnp.ones((pairs, LANES), F32)
+        scale = jnp.broadcast_to(square, one.shape)
+
+        whole, upper, lower, exact, small = on_grid(near)
+        exact, small = in_pieces(exact), in_pieces(small)
+        listed = dict(enumerate(exact + [one] * 3 + [-2.0 * v for v in whole]))
+        listed.update(enumerate(small + [one] * 3, SMALL))
+        for c in range(3):
+            n, m, l = -2.0 * whole[c], -2.0 * upper[c], -2.0 * lower[c]
+            listed.update(enumerate([n, n, m, l, m, m, l], SMALL + 6 + 7 * c))
+        listed.update(enumerate(near, COORDS))
+        for k, v in listed.items():
+            near_rows[t, pl.ds(k, pairs, stride=FEATURES), :] = v
+
+        whole, upper, lower, exact, small = on_grid(far)
+        small = small * square + 1.0
+        if t == TILES - 1:
+            valid = lax.broadcasted_iota(jnp.int32, small.shape, 1) < POINTS - t * LANES
+            small = jnp.where(valid, small, FAR_AWAY)
+        whole, upper, lower = [[v * square for v in part] for part in (whole, upper, lower)]
+        listed = dict(enumerate([scale] * 3 + in_pieces(exact * square) + whole))
+        listed.update(enumerate([scale] * 3 + in_pieces(small), SMALL))
+        for c in range(3):
+            n, m, l = whole[c], upper[c], lower[c]
+            listed.update(enumerate([m, l, n, n, m, l, m], SMALL + 6 + 7 * c))
+        for k, v in listed.items():
+            far_rows[t, pl.ds(k, pairs, stride=FEATURES), :] = v
+
+    def used(shape, axis, coords):
+        feature = lax.rem(lax.broadcasted_iota(jnp.int32, shape, axis), FEATURES)
+        keep = (feature < 9) | ((feature >= SMALL) & (feature < SMALL + 27))
+        if coords:
+            keep = keep | ((feature >= COORDS) & (feature < COORDS + 3))
+        return keep
+
+    near_used = used((LANES, LANES), 1, True)
+
+    def turn(t, carry):
+        start = pl.multiple_of(t * LANES, LANES)
+        for q in range(pairs // 2):
+            block = near_rows[t, q * LANES : (q + 1) * LANES, :].T
+            near_side[q, pl.ds(start, LANES), :] = jnp.where(near_used, block, 0.0)
+        return carry
+
+    lax.fori_loop(0, TILES, turn, 0)
     near_turned[...] = jnp.zeros_like(near_turned)
     force[...] = jnp.zeros_like(force)
 
     lane_wide = lax.broadcasted_iota(jnp.int32, (rows, LANES), 1)
-
-    def spread(pair, block):
-        start = pl.multiple_of(block * rows, 8)
-        columns = pltpu.roll(turned[pl.ds(start, rows), :], lax.rem(LANES - pair, LANES), 1)
-        for c in range(3):
-            column = columns[:, c * pairs : c * pairs + 1]
-            near_wide[c] = jnp.broadcast_to(column, (rows, LANES)).reshape(sub, 8, LANES)
-
-    def gather_near(pair, block):
-        start = pl.multiple_of(block * rows, 8)
-        value = near_turned[pl.ds(start, rows), :]
-        for c in range(3):
-            total = jnp.sum(near_sum[c].reshape(rows, LANES), axis=1, keepdims=True)
-            value = jnp.where(lane_wide == c * pairs + pair, total, value)
-        near_turned[pl.ds(start, rows), :] = value
+    far_used = used((FEATURES, LANES), 0, False)
 
     def one_pair(pair, carry):
+        group = pair // 2
+        odd = lax.rem(pair, 2)
+
+        def spread(block):
+            start = pl.multiple_of(block * rows, 8)
+            columns = pltpu.roll(
+                near_side[group, pl.ds(start, rows), :], lax.rem(LANES - odd * FEATURES, LANES), 1
+            )
+            for c in range(3):
+                column = columns[:, COORDS + c : COORDS + c + 1]
+                near_wide[c] = jnp.broadcast_to(column, (rows, LANES)).reshape(sub, 8, LANES)
+
+        def gather_near(block):
+            start = pl.multiple_of(block * rows, 8)
+            value = near_turned[pl.ds(start, rows), :]
+            for c in range(3):
+                total = jnp.sum(near_sum[c].reshape(rows, LANES), axis=1, keepdims=True)
+                value = jnp.where(lane_wide == c * pairs + pair, total, value)
+            near_turned[pl.ds(start, rows), :] = value
+
         for c in range(3):
             row = surface[pl.ds(c * 2 * pairs + pairs + pair, 1), :]
             far_wide[c] = jnp.broadcast_to(row, (8, PADDED))
+        for t in range(TILES):
+            start = pl.multiple_of(pair * FEATURES, FEATURES)
+            own = far_rows[t, pl.ds(start, FEATURES), :]
+            for side in range(2):
+                half_own = jnp.where(far_used & (odd == side), own, 0.0)
+                far_side[side * FEATURES : (side + 1) * FEATURES, t * LANES : (t + 1) * LANES] = (
+                    half_own.astype(BF16)
+                )
         far_sum[...] = jnp.zeros_like(far_sum)
         near_sum[...] = jnp.zeros_like(near_sum)
-        spread(pair, 0)
+        spread(0)
 
         def one_block(block, inner):
+            start = pl.multiple_of(block * rows, 8)
+            left = near_side[group, pl.ds(start, rows), :].astype(BF16)
             near = [near_wide[c] for c in range(3)]
-            gather_near(pair, jnp.maximum(block - 1, 0))
-            spread(pair, jnp.minimum(block + 1, blocks - 1))
+            gather_near(jnp.maximum(block - 1, 0))
+            spread(jnp.minimum(block + 1, blocks - 1))
             near_acc = [jnp.zeros((sub, 8, LANES), F32) for _ in range(3)]
-            for t in range(TILES):
-                lanes = slice(t * LANES, (t + 1) * LANES)
-                delta = [near[c] - far_wide[c, :, lanes][None] for c in range(3)]
-                grown = (delta[0] * delta[0] + delta[1] * delta[1]) + (delta[2] * delta[2] + 1.0)
-                kernel = 1.0 / grown
-                kernel = kernel * kernel
-                for c in range(3):
-                    pull = kernel * delta[c]
-                    near_acc[c] = near_acc[c] + pull
-                    far_sum[c, :, lanes] = far_sum[c, :, lanes] + jnp.sum(pull, axis=0)
+            for first in range(0, TILES, 2):
+                last = min(first + 2, TILES)
+                grown = jnp.dot(
+                    left,
+                    far_side[:, first * LANES : last * LANES],
+                    preferred_element_type=F32,
+                )
+                for t in range(first, last):
+                    lanes = slice(t * LANES, (t + 1) * LANES)
+                    here = slice((t - first) * LANES, (t - first + 1) * LANES)
+                    kernel = 1.0 / grown[:, here].reshape(sub, 8, LANES)
+                    kernel = kernel * kernel
+                    for c in range(3):
+                        pull = kernel * (near[c] - far_wide[c, :, lanes][None])
+                        near_acc[c] = near_acc[c] + pull
+                        far_sum[c, :, lanes] = far_sum[c, :, lanes] + jnp.sum(pull, axis=0)
             for c in range(3):
                 near_sum[c] = near_acc[c]
             return inner
 
         lax.fori_loop(0, blocks, one_block, 0)
-        gather_near(pair, blocks - 1)
+        gather_near(blocks - 1)
         for c in range(3):
             force[pl.ds(c * 2 * pairs + pairs + pair, 1), :] = -jnp.sum(
                 far_sum[c], axis=0, keepdims=True
@@ -341,10 +443,10 @@
     end_row = jnp.where(inside, end_slot, jnp.where(end_live, rim_row, 0))
     live_pairs = jnp.sum((pair_list[:, 0] >= 0).astype(jnp.int32))
     meta = jnp.concatenate([end_row, live_pairs[None]]).astype(jnp.int32)
-    offsets = jnp.pad(pair_offset.T, ((0, 0), (0, pairs))).reshape(-1, 1)
+    offsets = jnp.concatenate([pair_offset.T, -pair_offset.T], axis=1).reshape(-1, 1)
 
     lat, lon, weights = factor_tables()
-    rows = 96
+    rows = 192
     slot_force, low_force, high_force = pl.pallas_call(
         functools.partial(pair_kernel, slots, rows),
         out_shape=(
@@ -359,15 +461,18 @@
             pltpu.VMEM((2 * pairs * 8, LANES), F32),
             pltpu.VMEM((3 * LANES, PADDED), F32),
             pltpu.VMEM((6 * pairs, PADDED), F32),
-            pltpu.VMEM((PADDED, LANES), F32),
             pltpu.VMEM((6 * pairs, PADDED), F32),
             pltpu.VMEM((PADDED, LANES), F32),
+            pltpu.VMEM((TILES, pairs * FEATURES, LANES), F32),
+            pltpu.VMEM((pairs // 2, PADDED, LANES), F32),
+            pltpu.VMEM((TILES, pairs * FEATURES, LANES), F32),
+            pltpu.VMEM((2 * FEATURES, PADDED), BF16),
             pltpu.VMEM((3, 8, PADDED), F32),
             pltpu.VMEM((3, 8, PADDED), F32),
             pltpu.VMEM((3, rows // 8, 8, LANES), F32),
             pltpu.VMEM((3, rows // 8, 8, LANES), F32),
         ],
-        compiler_params=pltpu.CompilerParams(vmem_limit_bytes=48 << 20),
+        compiler_params=pltpu.CompilerParams(vmem_limit_bytes=56 << 20),
         name="pair_forces",
     )(
         meta,

time: 336 us -> 289 us (0.86)
  starting transfers between devices: 77.5 us -> 43 us
  Pallas kernels: 216 us -> 202 us
    all_to_all x1, starting transfers between devices: 52.1 us -> 17.6 us  [per_device(): lax.all_to_all(slot_force.reshape(members, slots.cap, 8, LANES), 'member'...]
    pallas_call x1, Pallas kernels: 211 us -> 198 us  [per_device(): pl.pallas_call(functools.partial(pair_kernel, slots, rows), out_shape=(ja...]
where the time goes in v2:
time: 289 us; the launch traced here: 287 us
  Pallas kernels  202 us (70%)
  starting transfers between devices  43 us (15%)
  waiting for transfers between devices  30.1 us (10%)
  local copies, waits for them, and re-layouts  8.18 us (3%)
  other arithmetic  3.66 us (1%)
    pallas_call x1, Pallas kernels, per_device(): pl.pallas_call(functools.partial(pair_kernel, slots, rows), out_shape=(ja...  198 us
    all_to_all x1, starting transfers between devices, per_device(): lax.all_to_all(slot_force.reshape(members, slots.cap, 8, LANES), 'member'...  17.6 us
    all_to_all x1, starting transfers between devices, per_device(): lax.all_to_all(request.reshape(members, slots.cap), 'member', split_axis=...  12.9 us
    all_to_all x1, waiting for transfers between devices, per_device(): lax.all_to_all(outgoing.reshape(members, slots.cap, 8, LANES), 'member',...  9.49 us
    all_to_all x1, waiting for transfers between devices, per_device(): lax.all_to_all(slot_force.reshape(members, slots.cap, 8, LANES), 'member'...  8.92 us
    all_to_all x1, waiting for transfers between devices, per_device(): lax.all_to_all(request.reshape(members, slots.cap), 'member', split_axis=...  7.37 us
  transfers between devices with their start and end apart: 7, of which 4 were waited for; matrix products, arithmetic and copies ran while one was open for 1% of the time, Pallas kernels for 0%

profile of v2, /device:TPU:8, one launch (start us, length us, event | category | flops | bytes accessed | tf_op | source)
XLA Modules:
  0.0 287.4 jit_solution(15651088289327116100)
XLA Ops:
  0.0 0.7 copy-done.7
  0.7 0.1 ne.116
  1.1 0.2 convert_reduce_fusion
  1.3 0.1 select_reduce_fusion
  1.3 0.8 all_to_all.12
  2.1 12.9 %all-to-all-start = ((s32[64,1,2]{2,1,0:T(1,128)}), s32[64,1,2]{2,1,0:T(1,128)S(1)}, u32[]{:S(2)}, u32[]{:S(2)}) async-start(s32[64,1,2]{2,1,0:T(1,128)} %bitcast.4), calls=%async_computation | async-start | bytes 65536 | tf_op jit(solution)/shard_map/all_to_all | solution.py:412
  15.1 0.7 slice-done
  15.8 0.1 reshape.170
  15.9 0.6 slice-done.1
  16.5 0.6 pad_maximum_fusion.tiles_ref
  17.2 7.4 %all-to-all-done = s32[64,1,2]{2,1,0:T(1,128)S(1)} async-done(((s32[64,1,2]{2,1,0:T(1,128)}), s32[64,1,2]{2,1,0:T(1,128)S(1)}, u32[]{:S(2)}, u32[]{:S(2)}) %all-to-all-start) | async-done | bytes 544 | tf_op jit(solution)/shard_map/all_to_all | solution.py:412
  24.5 0.5 broadcast.342
  25.0 0.7 reduce.4
  25.8 0.7 reshape.167.asked_ref
  26.4 1.8 pick.1
  28.3 5.4 %all-to-all-start.1 = ((f32[64,2,8,128]{3,2,1,0:T(8,128)}), f32[64,2,8,128]{3,2,1,0:T(8,128)S(1)}, u32[]{:S(2)}, u32[]{:S(2)}) async-start(f32[64,2,8,128]{3,2,1,0:T(8,128)} %bitcast.20), calls=%async_computation.1 | async-start | bytes 1048576 | tf_op jit(solution)/shard_map/all_to_all | solution.py:430
  33.7 1.3 collective-permute-start.1
  35.0 3.2 %collective-permute-start = (f32[4,8,128]{2,1,0:T(8,128)S(1)}, f32[4,8,128]{2,1,0:T(8,128)S(1)}, u32[]{:S(2)}, u32[]{:S(2)}) collective-permute-start(f32[4,8,128]{2,1,0:T(8,128)S(1)} %fusion), channel_id=1, source_target_pairs={{0,64},{64,128},{128,192},{1,65},{65,129},{129,193},{2,66},{66,130... | collective-permute-start | bytes 49160 | tf_op jit(solution)/shard_map/ppermute | solution.py:420
  38.4 0.6 fusion.6
  39.0 1.3 pad_add_fusion.meta_ref
  40.3 0.7 reshape.179.offset_ref
  41.0 9.5 %all-to-all-done.1 = f32[64,2,8,128]{3,2,1,0:T(8,128)S(1)} async-done(((f32[64,2,8,128]{3,2,1,0:T(8,128)}), f32[64,2,8,128]{3,2,1,0:T(8,128)S(1)}, u32[]{:S(2)}, u32[]{:S(2)}) %all-to-all-start.1) | async-done | bytes 524320 | tf_op jit(solution)/shard_map/all_to_all | solution.py:430
  50.5 0.8 copy-done
  51.3 197.9 %pair_forces.1 = (f32[1024,128]{1,0:T(8,128)}, f32[32,128]{1,0:T(8,128)}, f32[32,128]{1,0:T(8,128)}) custom-call(s32[33]{0:T(128)} %pad_add_fusion.meta_ref, f32[96,1]{1,0:T(8,128)} %reshape.179.offset_ref, f32[384,128]{1,0:T(8,128)} %constant.91.clone.lat_ref, f32[384,128]{1,0:T(8,128)} %constant.92.clone.lon_ref, f32[8,2176]{1,0:T(8,128)} %constant.93.clone.weight_ref, ...), custom_call_target="tpu_custom_call" | custom-call | tf_op jit(solution)/shard_map/pair_forces/pallas_call | solution.py:450
  249.2 17.6 %all-to-all-start.2 = ((f32[64,2,8,128]{3,2,1,0:T(8,128)}), f32[64,2,8,128]{3,2,1,0:T(8,128)S(1)}, u32[]{:S(2)}, u32[]{:S(2)}) async-start(f32[64,2,8,128]{3,2,1,0:T(8,128)} %bitcast.23), calls=%async_computation.2 | async-start | bytes 1048576 | tf_op jit(solution)/shard_map/all_to_all | solution.py:487
  266.8 1.3 collective-permute-start.2
  268.1 1.3 collective-permute-start.3
  269.4 4.3 %collective-permute-done.3.high_ref = f32[4,8,128]{2,1,0:T(8,128)S(1)} collective-permute-done((f32[4,8,128]{2,1,0:T(8,128)S(1)}, f32[4,8,128]{2,1,0:T(8,128)S(1)}, u32[]{:S(2)}, u32[]{:S(2)}) %collective-permute-start.3) | collective-permute-done | bytes 16416 | tf_op jit(solution)/shard_map/ppermute | solution.py:495
  273.8 8.9 %all-to-all-done.2 = f32[64,2,8,128]{3,2,1,0:T(8,128)S(1)} async-done(((f32[64,2,8,128]{3,2,1,0:T(8,128)}), f32[64,2,8,128]{3,2,1,0:T(8,128)S(1)}, u32[]{:S(2)}, u32[]{:S(2)}) %all-to-all-start.2) | async-done | bytes 524320 | tf_op jit(solution)/shard_map/all_to_all | solution.py:487
  282.7 0.8 copy-done.1
  283.5 2.5 collect.1
  286.0 1.4 copy.24
  (36 shorter events, 0.5 us)
Async XLA Ops:
  0.0 0.7 copy-start.7
  2.1 22.4 %all-to-all-start = ((s32[64,1,2]{2,1,0:T(1,128)}), s32[64,1,2]{2,1,0:T(1,128)S(1)}, u32[]{:S(2)}, u32[]{:S(2)}) async-start(s32[64,1,2]{2,1,0:T(1,128)} %bitcast.4), calls=%async_computation | async-start | bytes 65536 | tf_op jit(solution)/shard_map/all_to_all | solution.py:412
  15.1 0.7 slice-start
  15.8 0.7 slice-start.1
  28.3 22.2 %all-to-all-start.1 = ((f32[64,2,8,128]{3,2,1,0:T(8,128)}), f32[64,2,8,128]{3,2,1,0:T(8,128)S(1)}, u32[]{:S(2)}, u32[]{:S(2)}) async-start(f32[64,2,8,128]{3,2,1,0:T(8,128)} %bitcast.20), calls=%async_computation.1 | async-start | bytes 1048576 | tf_op jit(solution)/shard_map/all_to_all | solution.py:430
  33.7 4.5 %copy-start.6 = (f32[16,3]{0,1:T(4,128)S(1)}, f32[16,3]{0,1:T(4,128)}, u32[]{:S(2)}) copy-start(f32[16,3]{0,1:T(4,128)} %param.8) | copy-start | bytes 580
  33.7 7.3 %collective-permute-start.1 = (f32[4,8,128]{2,1,0:T(8,128)S(1)}, f32[4,8,128]{2,1,0:T(8,128)S(1)}, u32[]{:S(2)}, u32[]{:S(2)}) collective-permute-start(f32[4,8,128]{2,1,0:T(8,128)S(1)} %fusion), channel_id=1, source_target_pairs={{64,0},{128,64},{192,128},{65,1},{129,65},{193,129},{66,2},{130,66... | collective-permute-start | bytes 49160 | tf_op jit(solution)/shard_map/ppermute | solution.py:421
  35.0 6.0 %collective-permute-start = (f32[4,8,128]{2,1,0:T(8,128)S(1)}, f32[4,8,128]{2,1,0:T(8,128)S(1)}, u32[]{:S(2)}, u32[]{:S(2)}) collective-permute-start(f32[4,8,128]{2,1,0:T(8,128)S(1)} %fusion), channel_id=1, source_target_pairs={{0,64},{64,128},{128,192},{1,65},{65,129},{129,193},{2,66},{66,130... | collective-permute-start | bytes 49160 | tf_op jit(solution)/shard_map/ppermute | solution.py:420
  41.0 9.5 %copy-start.2 = (f32[4,8,128]{2,1,0:T(8,128)}, f32[4,8,128]{2,1,0:T(8,128)S(1)}, u32[]{:S(2)}) copy-start(f32[4,8,128]{2,1,0:T(8,128)S(1)} %collective-permute-done.1) | copy-start | bytes 49156
  41.0 9.5 %copy-start.3 = (f32[4,8,128]{2,1,0:T(8,128)}, f32[4,8,128]{2,1,0:T(8,128)S(1)}, u32[]{:S(2)}) copy-start(f32[4,8,128]{2,1,0:T(8,128)S(1)} %collective-permute-done) | copy-start | bytes 49156
  50.5 0.8 copy-start
  249.2 17.6 %copy-start.9 = (f32[32,128]{1,0:T(8,128)S(1)}, f32[32,128]{1,0:T(8,128)}, u32[]{:S(2)}) copy-start(f32[32,128]{1,0:T(8,128)} %get-tuple-element.9) | copy-start | bytes 49156
  249.2 18.9 %copy-start.8 = (f32[32,128]{1,0:T(8,128)S(1)}, f32[32,128]{1,0:T(8,128)}, u32[]{:S(2)}) copy-start(f32[32,128]{1,0:T(8,128)} %get-tuple-element.10) | copy-start | bytes 49156
  249.2 33.5 %all-to-all-start.2 = ((f32[64,2,8,128]{3,2,1,0:T(8,128)}), f32[64,2,8,128]{3,2,1,0:T(8,128)S(1)}, u32[]{:S(2)}, u32[]{:S(2)}) async-start(f32[64,2,8,128]{3,2,1,0:T(8,128)} %bitcast.23), calls=%async_computation.2 | async-start | bytes 1048576 | tf_op jit(solution)/shard_map/all_to_all | solution.py:487
  266.8 2.6 collective-permute-start.2
  268.1 5.7 %collective-permute-start.3 = (f32[4,8,128]{2,1,0:T(8,128)S(1)}, f32[4,8,128]{2,1,0:T(8,128)S(1)}, u32[]{:S(2)}, u32[]{:S(2)}) collective-permute-start(f32[4,8,128]{2,1,0:T(8,128)S(1)} %bitcast.27), channel_id=1, source_target_pairs={{64,0},{128,64},{192,128},{65,1},{129,65},{193,129},{66,2},{130,66... | collective-permute-start | bytes 49160 | tf_op jit(solution)/shard_map/ppermute | solution.py:495
  269.4 13.3 %copy-start.4 = (f32[4,8,128]{2,1,0:T(8,128)}, f32[4,8,128]{2,1,0:T(8,128)S(1)}, u32[]{:S(2)}) copy-start(f32[4,8,128]{2,1,0:T(8,128)S(1)} %collective-permute-done.2.low_ref) | copy-start | bytes 49156
  273.8 8.9 %copy-start.5 = (f32[4,8,128]{2,1,0:T(8,128)}, f32[4,8,128]{2,1,0:T(8,128)S(1)}, u32[]{:S(2)}) copy-start(f32[4,8,128]{2,1,0:T(8,128)S(1)} %collective-permute-done.3.high_ref) | copy-start | bytes 49156
  282.7 0.8 copy-start.1

commit v3 on v2

--- a/solution.py
+++ b/solution.py
@@ -176,6 +176,15 @@
         small = [2.0 * w * r + r * r for w, r in zip(whole, rest)]
         return whole, upper, lower, exact, small[0] + small[1] + small[2]
 
+    def used(shape, axis, coords):
+        feature = lax.rem(lax.broadcasted_iota(jnp.int32, shape, axis), FEATURES)
+        keep = (feature < 9) | ((feature >= SMALL) & (feature < SMALL + 27))
+        if coords:
+            keep = keep | ((feature >= COORDS) & (feature < COORDS + 3))
+        return keep
+
+    near_used = used((LANES, LANES), 1, True)
+
     for t in range(TILES):
         lanes = slice(t * LANES, (t + 1) * LANES)
         near = [surface[c * 2 * pairs : c * 2 * pairs + pairs, lanes] for c in range(3)]
@@ -193,6 +202,9 @@
         listed.update(enumerate(near, COORDS))
         for k, v in listed.items():
             near_rows[t, pl.ds(k, pairs, stride=FEATURES), :] = v
+        for q in range(pairs // 2):
+            block = near_rows[t, q * LANES : (q + 1) * LANES, :].T
+            near_side[q, lanes, :] = jnp.where(near_used, block, 0.0)
 
         whole, upper, lower, exact, small = on_grid(far)
         small = small * square + 1.0
@@ -208,23 +220,6 @@
         for k, v in listed.items():
             far_rows[t, pl.ds(k, pairs, stride=FEATURES), :] = v
 
-    def used(shape, axis, coords):
-        feature = lax.rem(lax.broadcasted_iota(jnp.int32, shape, axis), FEATURES)
-        keep = (feature < 9) | ((feature >= SMALL) & (feature < SMALL + 27))
-        if coords:
-            keep = keep | ((feature >= COORDS) & (feature < COORDS + 3))
-        return keep
-
-    near_used = used((LANES, LANES), 1, True)
-
-    def turn(t, carry):
-        start = pl.multiple_of(t * LANES, LANES)
-        for q in range(pairs // 2):
-            block = near_rows[t, q * LANES : (q + 1) * LANES, :].T
-            near_side[q, pl.ds(start, LANES), :] = jnp.where(near_used, block, 0.0)
-        return carry
-
-    lax.fori_loop(0, TILES, turn, 0)
     near_turned[...] = jnp.zeros_like(near_turned)
     force[...] = jnp.zeros_like(force)
 
@@ -446,7 +441,7 @@
     offsets = jnp.concatenate([pair_offset.T, -pair_offset.T], axis=1).reshape(-1, 1)
 
     lat, lon, weights = factor_tables()
-    rows = 192
+    rows = 264
     slot_force, low_force, high_force = pl.pallas_call(
         functools.partial(pair_kernel, slots, rows),
         out_shape=(

time: 289 us -> 284 us (0.983)
  Pallas kernels: 202 us -> 198 us
    pallas_call x1, Pallas kernels: 198 us -> 194 us  [per_device(): pl.pallas_call(functools.partial(pair_kernel, slots, rows), out_shape=(ja...]
where the time goes in v3:
time: 284 us; the launch traced here: 283 us
  Pallas kernels  198 us (70%)
  starting transfers between devices  42.7 us (15%)
  waiting for transfers between devices  30.5 us (11%)
  local copies, waits for them, and re-layouts  8.18 us (3%)
  other arithmetic  3.66 us (1%)
    pallas_call x1, Pallas kernels, per_device(): pl.pallas_call(functools.partial(pair_kernel, slots, rows), out_shape=(ja...  194 us
    all_to_all x1, starting transfers between devices, per_device(): lax.all_to_all(slot_force.reshape(members, slots.cap, 8, LANES), 'member'...  17.3 us
    all_to_all x1, starting transfers between devices, per_device(): lax.all_to_all(request.reshape(members, slots.cap), 'member', split_axis=...  12.9 us
    all_to_all x1, waiting for transfers between devices, per_device(): lax.all_to_all(outgoing.reshape(members, slots.cap, 8, LANES), 'member',...  9.49 us
    all_to_all x1, waiting for transfers between devices, per_device(): lax.all_to_all(slot_force.reshape(members, slots.cap, 8, LANES), 'member'...  9.25 us
    all_to_all x1, waiting for transfers between devices, per_device(): lax.all_to_all(request.reshape(members, slots.cap), 'member', split_axis=...  7.37 us
  transfers between devices with their start and end apart: 7, of which 4 were waited for; matrix products, arithmetic and copies ran while one was open for 1% of the time, Pallas kernels for 0%

profile of v3, /device:TPU:8, one launch (start us, length us, event | category | flops | bytes accessed | tf_op | source)
XLA Modules:
  0.0 283.1 jit_solution(813040877994376791)
XLA Ops:
  0.0 0.7 copy-done.7
  0.7 0.1 ne.116
  1.1 0.2 convert_reduce_fusion
  1.3 0.1 select_reduce_fusion
  1.3 0.8 all_to_all.12
  2.1 12.9 %all-to-all-start = ((s32[64,1,2]{2,1,0:T(1,128)}), s32[64,1,2]{2,1,0:T(1,128)S(1)}, u32[]{:S(2)}, u32[]{:S(2)}) async-start(s32[64,1,2]{2,1,0:T(1,128)} %bitcast.4), calls=%async_computation | async-start | bytes 65536 | tf_op jit(solution)/shard_map/all_to_all | solution.py:407
  15.1 0.7 slice-done
  15.8 0.1 reshape.170
  15.9 0.6 slice-done.1
  16.5 0.6 pad_maximum_fusion.tiles_ref
  17.2 7.4 %all-to-all-done = s32[64,1,2]{2,1,0:T(1,128)S(1)} async-done(((s32[64,1,2]{2,1,0:T(1,128)}), s32[64,1,2]{2,1,0:T(1,128)S(1)}, u32[]{:S(2)}, u32[]{:S(2)}) %all-to-all-start) | async-done | bytes 544 | tf_op jit(solution)/shard_map/all_to_all | solution.py:407
  24.5 0.5 broadcast.342
  25.0 0.7 reduce.4
  25.8 0.7 reshape.167.asked_ref
  26.4 1.8 pick.1
  28.3 5.4 %all-to-all-start.1 = ((f32[64,2,8,128]{3,2,1,0:T(8,128)}), f32[64,2,8,128]{3,2,1,0:T(8,128)S(1)}, u32[]{:S(2)}, u32[]{:S(2)}) async-start(f32[64,2,8,128]{3,2,1,0:T(8,128)} %bitcast.20), calls=%async_computation.1 | async-start | bytes 1048576 | tf_op jit(solution)/shard_map/all_to_all | solution.py:425
  33.7 1.3 collective-permute-start.1
  35.0 3.2 %collective-permute-start = (f32[4,8,128]{2,1,0:T(8,128)S(1)}, f32[4,8,128]{2,1,0:T(8,128)S(1)}, u32[]{:S(2)}, u32[]{:S(2)}) collective-permute-start(f32[4,8,128]{2,1,0:T(8,128)S(1)} %fusion), channel_id=1, source_target_pairs={{0,64},{64,128},{128,192},{1,65},{65,129},{129,193},{2,66},{66,130... | collective-permute-start | bytes 49160 | tf_op jit(solution)/shard_map/ppermute | solution.py:415
  38.4 0.6 fusion.6
  39.0 1.3 pad_add_fusion.meta_ref
  40.3 0.7 reshape.179.offset_ref
  41.0 9.5 %all-to-all-done.1 = f32[64,2,8,128]{3,2,1,0:T(8,128)S(1)} async-done(((f32[64,2,8,128]{3,2,1,0:T(8,128)}), f32[64,2,8,128]{3,2,1,0:T(8,128)S(1)}, u32[]{:S(2)}, u32[]{:S(2)}) %all-to-all-start.1) | async-done | bytes 524320 | tf_op jit(solution)/shard_map/all_to_all | solution.py:425
  50.5 0.8 copy-done
  51.3 193.5 %pair_forces.1 = (f32[1024,128]{1,0:T(8,128)}, f32[32,128]{1,0:T(8,128)}, f32[32,128]{1,0:T(8,128)}) custom-call(s32[33]{0:T(128)} %pad_add_fusion.meta_ref, f32[96,1]{1,0:T(8,128)} %reshape.179.offset_ref, f32[384,128]{1,0:T(8,128)} %constant.91.clone.lat_ref, f32[384,128]{1,0:T(8,128)} %constant.92.clone.lon_ref, f32[8,2176]{1,0:T(8,128)} %constant.93.clone.weight_ref, ...), custom_call_target="tpu_custom_call" | custom-call | tf_op jit(solution)/shard_map/pair_forces/pallas_call | solution.py:445
  244.8 17.3 %all-to-all-start.2 = ((f32[64,2,8,128]{3,2,1,0:T(8,128)}), f32[64,2,8,128]{3,2,1,0:T(8,128)S(1)}, u32[]{:S(2)}, u32[]{:S(2)}) async-start(f32[64,2,8,128]{3,2,1,0:T(8,128)} %bitcast.23), calls=%async_computation.2 | async-start | bytes 1048576 | tf_op jit(solution)/shard_map/all_to_all | solution.py:482
  262.1 1.3 collective-permute-start.2
  263.4 1.3 collective-permute-start.3
  264.7 4.4 %collective-permute-done.3.high_ref = f32[4,8,128]{2,1,0:T(8,128)S(1)} collective-permute-done((f32[4,8,128]{2,1,0:T(8,128)S(1)}, f32[4,8,128]{2,1,0:T(8,128)S(1)}, u32[]{:S(2)}, u32[]{:S(2)}) %collective-permute-start.3) | collective-permute-done | bytes 16416 | tf_op jit(solution)/shard_map/ppermute | solution.py:490
  269.1 9.2 %all-to-all-done.2 = f32[64,2,8,128]{3,2,1,0:T(8,128)S(1)} async-done(((f32[64,2,8,128]{3,2,1,0:T(8,128)}), f32[64,2,8,128]{3,2,1,0:T(8,128)S(1)}, u32[]{:S(2)}, u32[]{:S(2)}) %all-to-all-start.2) | async-done | bytes 524320 | tf_op jit(solution)/shard_map/all_to_all | solution.py:482
  278.4 0.8 copy-done.1
  279.2 2.5 collect.1
  281.6 1.4 copy.24
  (36 shorter events, 0.5 us)
Async XLA Ops:
  0.0 0.7 copy-start.7
  2.1 22.4 %all-to-all-start = ((s32[64,1,2]{2,1,0:T(1,128)}), s32[64,1,2]{2,1,0:T(1,128)S(1)}, u32[]{:S(2)}, u32[]{:S(2)}) async-start(s32[64,1,2]{2,1,0:T(1,128)} %bitcast.4), calls=%async_computation | async-start | bytes 65536 | tf_op jit(solution)/shard_map/all_to_all | solution.py:407
  15.1 0.7 slice-start
  15.8 0.7 slice-start.1
  28.3 22.2 %all-to-all-start.1 = ((f32[64,2,8,128]{3,2,1,0:T(8,128)}), f32[64,2,8,128]{3,2,1,0:T(8,128)S(1)}, u32[]{:S(2)}, u32[]{:S(2)}) async-start(f32[64,2,8,128]{3,2,1,0:T(8,128)} %bitcast.20), calls=%async_computation.1 | async-start | bytes 1048576 | tf_op jit(solution)/shard_map/all_to_all | solution.py:425
  33.7 4.5 %copy-start.6 = (f32[16,3]{0,1:T(4,128)S(1)}, f32[16,3]{0,1:T(4,128)}, u32[]{:S(2)}) copy-start(f32[16,3]{0,1:T(4,128)} %param.8) | copy-start | bytes 580
  33.7 7.3 %collective-permute-start.1 = (f32[4,8,128]{2,1,0:T(8,128)S(1)}, f32[4,8,128]{2,1,0:T(8,128)S(1)}, u32[]{:S(2)}, u32[]{:S(2)}) collective-permute-start(f32[4,8,128]{2,1,0:T(8,128)S(1)} %fusion), channel_id=1, source_target_pairs={{64,0},{128,64},{192,128},{65,1},{129,65},{193,129},{66,2},{130,66... | collective-permute-start | bytes 49160 | tf_op jit(solution)/shard_map/ppermute | solution.py:416
  35.0 6.0 %collective-permute-start = (f32[4,8,128]{2,1,0:T(8,128)S(1)}, f32[4,8,128]{2,1,0:T(8,128)S(1)}, u32[]{:S(2)}, u32[]{:S(2)}) collective-permute-start(f32[4,8,128]{2,1,0:T(8,128)S(1)} %fusion), channel_id=1, source_target_pairs={{0,64},{64,128},{128,192},{1,65},{65,129},{129,193},{2,66},{66,130... | collective-permute-start | bytes 49160 | tf_op jit(solution)/shard_map/ppermute | solution.py:415
  41.0 9.5 %copy-start.2 = (f32[4,8,128]{2,1,0:T(8,128)}, f32[4,8,128]{2,1,0:T(8,128)S(1)}, u32[]{:S(2)}) copy-start(f32[4,8,128]{2,1,0:T(8,128)S(1)} %collective-permute-done.1) | copy-start | bytes 49156
  41.0 9.5 %copy-start.3 = (f32[4,8,128]{2,1,0:T(8,128)}, f32[4,8,128]{2,1,0:T(8,128)S(1)}, u32[]{:S(2)}) copy-start(f32[4,8,128]{2,1,0:T(8,128)S(1)} %collective-permute-done) | copy-start | bytes 49156
  50.5 0.8 copy-start
  244.8 17.3 %copy-start.9 = (f32[32,128]{1,0:T(8,128)S(1)}, f32[32,128]{1,0:T(8,128)}, u32[]{:S(2)}) copy-start(f32[32,128]{1,0:T(8,128)} %get-tuple-element.9) | copy-start | bytes 49156
  244.8 18.6 %copy-start.8 = (f32[32,128]{1,0:T(8,128)S(1)}, f32[32,128]{1,0:T(8,128)}, u32[]{:S(2)}) copy-start(f32[32,128]{1,0:T(8,128)} %get-tuple-element.10) | copy-start | bytes 49156
  244.8 33.5 %all-to-all-start.2 = ((f32[64,2,8,128]{3,2,1,0:T(8,128)}), f32[64,2,8,128]{3,2,1,0:T(8,128)S(1)}, u32[]{:S(2)}, u32[]{:S(2)}) async-start(f32[64,2,8,128]{3,2,1,0:T(8,128)} %bitcast.23), calls=%async_computation.2 | async-start | bytes 1048576 | tf_op jit(solution)/shard_map/all_to_all | solution.py:482
  262.1 2.6 collective-permute-start.2
  263.4 5.7 %collective-permute-start.3 = (f32[4,8,128]{2,1,0:T(8,128)S(1)}, f32[4,8,128]{2,1,0:T(8,128)S(1)}, u32[]{:S(2)}, u32[]{:S(2)}) collective-permute-start(f32[4,8,128]{2,1,0:T(8,128)S(1)} %bitcast.27), channel_id=1, source_target_pairs={{64,0},{128,64},{192,128},{65,1},{129,65},{193,129},{66,2},{130,66... | collective-permute-start | bytes 49160 | tf_op jit(solution)/shard_map/ppermute | solution.py:490
  264.7 13.6 %copy-start.4 = (f32[4,8,128]{2,1,0:T(8,128)}, f32[4,8,128]{2,1,0:T(8,128)S(1)}, u32[]{:S(2)}) copy-start(f32[4,8,128]{2,1,0:T(8,128)S(1)} %collective-permute-done.2.low_ref) | copy-start | bytes 49156
  269.1 9.3 %copy-start.5 = (f32[4,8,128]{2,1,0:T(8,128)}, f32[4,8,128]{2,1,0:T(8,128)S(1)}, u32[]{:S(2)}) copy-start(f32[4,8,128]{2,1,0:T(8,128)S(1)} %collective-permute-done.3.high_ref) | copy-start | bytes 49156
  278.4 0.8 copy-start.1

commit v4 on v3

--- a/solution.py
+++ b/solution.py
@@ -184,6 +184,8 @@
         return keep
 
     near_used = used((LANES, LANES), 1, True)
+    feature = lax.rem(lax.broadcasted_iota(jnp.int32, (LANES, LANES), 1), FEATURES)
+    near_one = ((feature >= 3) & (feature < 6)) | ((feature >= SMALL + 3) & (feature < SMALL + 6))
 
     for t in range(TILES):
         lanes = slice(t * LANES, (t + 1) * LANES)
@@ -194,8 +196,9 @@
 
         whole, upper, lower, exact, small = on_grid(near)
         exact, small = in_pieces(exact), in_pieces(small)
-        listed = dict(enumerate(exact + [one] * 3 + [-2.0 * v for v in whole]))
-        listed.update(enumerate(small + [one] * 3, SMALL))
+        listed = dict(enumerate(exact))
+        listed.update(enumerate([-2.0 * v for v in whole], 6))
+        listed.update(enumerate(small, SMALL))
         for c in range(3):
             n, m, l = -2.0 * whole[c], -2.0 * upper[c], -2.0 * lower[c]
             listed.update(enumerate([n, n, m, l, m, m, l], SMALL + 6 + 7 * c))
@@ -204,7 +207,7 @@
             near_rows[t, pl.ds(k, pairs, stride=FEATURES), :] = v
         for q in range(pairs // 2):
             block = near_rows[t, q * LANES : (q + 1) * LANES, :].T
-            near_side[q, lanes, :] = jnp.where(near_used, block, 0.0)
+            near_side[q, lanes, :] = jnp.where(near_one, 1.0, jnp.where(near_used, block, 0.0))
 
         whole, upper, lower, exact, small = on_grid(far)
         small = small * square + 1.0

time: 284 us -> 283 us (level)
  Pallas kernels: 198 us -> 186 us
  starting transfers between devices: 42.7 us -> 54.3 us
    pallas_call x1, Pallas kernels: 194 us -> 181 us  [per_device(): pl.pallas_call(functools.partial(pair_kernel, slots, rows), out_shape=(ja...]
    all_to_all x1, starting transfers between devices: 17.3 us -> 28.8 us  [per_device(): lax.all_to_all(slot_force.reshape(members, slots.cap, 8, LANES), 'member'...]
where the time goes in v4:
time: 283 us
  Pallas kernels  186 us (66%)
  starting transfers between devices  54.3 us (19%)
  waiting for transfers between devices  30.7 us (11%)
  local copies, waits for them, and re-layouts  8.18 us (3%)
  other arithmetic  3.66 us (1%)
    pallas_call x1, Pallas kernels, per_device(): pl.pallas_call(functools.partial(pair_kernel, slots, rows), out_shape=(ja...  181 us
    all_to_all x1, starting transfers between devices, per_device(): lax.all_to_all(slot_force.reshape(members, slots.cap, 8, LANES), 'member'...  28.8 us
    all_to_all x1, starting transfers between devices, per_device(): lax.all_to_all(request.reshape(members, slots.cap), 'member', split_axis=...  12.9 us
    all_to_all x1, waiting for transfers between devices, per_device(): lax.all_to_all(slot_force.reshape(members, slots.cap, 8, LANES), 'member'...  9.78 us
    all_to_all x1, waiting for transfers between devices, per_device(): lax.all_to_all(outgoing.reshape(members, slots.cap, 8, LANES), 'member',...  9.49 us
    all_to_all x1, waiting for transfers between devices, per_device(): lax.all_to_all(request.reshape(members, slots.cap), 'member', split_axis=...  7.37 us
  transfers between devices with their start and end apart: 7, of which 4 were waited for; matrix products, arithmetic and copies ran while one was open for 1% of the time, Pallas kernels for 0%

profile of v4, /device:TPU:8, one launch (start us, length us, event | category | flops | bytes accessed | tf_op | source)
XLA Modules:
  0.0 282.6 jit_solution(13146375273036968748)
XLA Ops:
  0.0 0.7 copy-done.7
  0.7 0.1 ne.116
  1.1 0.2 convert_reduce_fusion
  1.3 0.1 select_reduce_fusion
  1.3 0.8 all_to_all.12
  2.1 12.9 %all-to-all-start = ((s32[64,1,2]{2,1,0:T(1,128)}), s32[64,1,2]{2,1,0:T(1,128)S(1)}, u32[]{:S(2)}, u32[]{:S(2)}) async-start(s32[64,1,2]{2,1,0:T(1,128)} %bitcast.4), calls=%async_computation | async-start | bytes 65536 | tf_op jit(solution)/shard_map/all_to_all | solution.py:410
  15.1 0.7 slice-done
  15.8 0.1 reshape.170
  15.9 0.6 slice-done.1
  16.5 0.6 pad_maximum_fusion.tiles_ref
  17.2 7.4 %all-to-all-done = s32[64,1,2]{2,1,0:T(1,128)S(1)} async-done(((s32[64,1,2]{2,1,0:T(1,128)}), s32[64,1,2]{2,1,0:T(1,128)S(1)}, u32[]{:S(2)}, u32[]{:S(2)}) %all-to-all-start) | async-done | bytes 544 | tf_op jit(solution)/shard_map/all_to_all | solution.py:410
  24.5 0.5 broadcast.342
  25.0 0.7 reduce.4
  25.8 0.7 reshape.167.asked_ref
  26.4 1.8 pick.1
  28.3 5.4 %all-to-all-start.1 = ((f32[64,2,8,128]{3,2,1,0:T(8,128)}), f32[64,2,8,128]{3,2,1,0:T(8,128)S(1)}, u32[]{:S(2)}, u32[]{:S(2)}) async-start(f32[64,2,8,128]{3,2,1,0:T(8,128)} %bitcast.20), calls=%async_computation.1 | async-start | bytes 1048576 | tf_op jit(solution)/shard_map/all_to_all | solution.py:428
  33.7 1.3 collective-permute-start.1
  35.0 3.2 %collective-permute-start = (f32[4,8,128]{2,1,0:T(8,128)S(1)}, f32[4,8,128]{2,1,0:T(8,128)S(1)}, u32[]{:S(2)}, u32[]{:S(2)}) collective-permute-start(f32[4,8,128]{2,1,0:T(8,128)S(1)} %fusion), channel_id=1, source_target_pairs={{0,64},{64,128},{128,192},{1,65},{65,129},{129,193},{2,66},{66,130... | collective-permute-start | bytes 49160 | tf_op jit(solution)/shard_map/ppermute | solution.py:418
  38.4 0.6 fusion.6
  39.0 1.3 pad_add_fusion.meta_ref
  40.3 0.7 reshape.179.offset_ref
  41.0 9.5 %all-to-all-done.1 = f32[64,2,8,128]{3,2,1,0:T(8,128)S(1)} async-done(((f32[64,2,8,128]{3,2,1,0:T(8,128)}), f32[64,2,8,128]{3,2,1,0:T(8,128)S(1)}, u32[]{:S(2)}, u32[]{:S(2)}) %all-to-all-start.1) | async-done | bytes 524320 | tf_op jit(solution)/shard_map/all_to_all | solution.py:428
  50.5 0.8 copy-done
  51.3 181.2 %pair_forces.1 = (f32[1024,128]{1,0:T(8,128)}, f32[32,128]{1,0:T(8,128)}, f32[32,128]{1,0:T(8,128)}) custom-call(s32[33]{0:T(128)} %pad_add_fusion.meta_ref, f32[96,1]{1,0:T(8,128)} %reshape.179.offset_ref, f32[384,128]{1,0:T(8,128)} %constant.91.clone.lat_ref, f32[384,128]{1,0:T(8,128)} %constant.92.clone.lon_ref, f32[8,2176]{1,0:T(8,128)} %constant.93.clone.weight_ref, ...), custom_call_target="tpu_custom_call" | custom-call | tf_op jit(solution)/shard_map/pair_forces/pallas_call | solution.py:448
  232.6 28.8 %all-to-all-start.2 = ((f32[64,2,8,128]{3,2,1,0:T(8,128)}), f32[64,2,8,128]{3,2,1,0:T(8,128)S(1)}, u32[]{:S(2)}, u32[]{:S(2)}) async-start(f32[64,2,8,128]{3,2,1,0:T(8,128)} %bitcast.23), calls=%async_computation.2 | async-start | bytes 1048576 | tf_op jit(solution)/shard_map/all_to_all | solution.py:485
  261.4 1.3 collective-permute-start.2
  262.7 1.3 collective-permute-start.3
  264.0 4.0 %collective-permute-done.3.high_ref = f32[4,8,128]{2,1,0:T(8,128)S(1)} collective-permute-done((f32[4,8,128]{2,1,0:T(8,128)S(1)}, f32[4,8,128]{2,1,0:T(8,128)S(1)}, u32[]{:S(2)}, u32[]{:S(2)}) %collective-permute-start.3) | collective-permute-done | bytes 16416 | tf_op jit(solution)/shard_map/ppermute | solution.py:493
  268.1 9.8 %all-to-all-done.2 = f32[64,2,8,128]{3,2,1,0:T(8,128)S(1)} async-done(((f32[64,2,8,128]{3,2,1,0:T(8,128)}), f32[64,2,8,128]{3,2,1,0:T(8,128)S(1)}, u32[]{:S(2)}, u32[]{:S(2)}) %all-to-all-start.2) | async-done | bytes 524320 | tf_op jit(solution)/shard_map/all_to_all | solution.py:485
  277.9 0.8 copy-done.1
  278.6 2.5 collect.1
  281.2 1.4 copy.24
  (36 shorter events, 0.5 us)
Async XLA Ops:
  0.0 0.7 copy-start.7
  2.1 22.4 %all-to-all-start = ((s32[64,1,2]{2,1,0:T(1,128)}), s32[64,1,2]{2,1,0:T(1,128)S(1)}, u32[]{:S(2)}, u32[]{:S(2)}) async-start(s32[64,1,2]{2,1,0:T(1,128)} %bitcast.4), calls=%async_computation | async-start | bytes 65536 | tf_op jit(solution)/shard_map/all_to_all | solution.py:410
  15.1 0.7 slice-start
  15.8 0.7 slice-start.1
  28.3 22.2 %all-to-all-start.1 = ((f32[64,2,8,128]{3,2,1,0:T(8,128)}), f32[64,2,8,128]{3,2,1,0:T(8,128)S(1)}, u32[]{:S(2)}, u32[]{:S(2)}) async-start(f32[64,2,8,128]{3,2,1,0:T(8,128)} %bitcast.20), calls=%async_computation.1 | async-start | bytes 1048576 | tf_op jit(solution)/shard_map/all_to_all | solution.py:428
  33.7 4.5 %copy-start.6 = (f32[16,3]{0,1:T(4,128)S(1)}, f32[16,3]{0,1:T(4,128)}, u32[]{:S(2)}) copy-start(f32[16,3]{0,1:T(4,128)} %param.8) | copy-start | bytes 580
  33.7 7.3 %collective-permute-start.1 = (f32[4,8,128]{2,1,0:T(8,128)S(1)}, f32[4,8,128]{2,1,0:T(8,128)S(1)}, u32[]{:S(2)}, u32[]{:S(2)}) collective-permute-start(f32[4,8,128]{2,1,0:T(8,128)S(1)} %fusion), channel_id=1, source_target_pairs={{64,0},{128,64},{192,128},{65,1},{129,65},{193,129},{66,2},{130,66... | collective-permute-start | bytes 49160 | tf_op jit(solution)/shard_map/ppermute | solution.py:419
  35.0 6.0 %collective-permute-start = (f32[4,8,128]{2,1,0:T(8,128)S(1)}, f32[4,8,128]{2,1,0:T(8,128)S(1)}, u32[]{:S(2)}, u32[]{:S(2)}) collective-permute-start(f32[4,8,128]{2,1,0:T(8,128)S(1)} %fusion), channel_id=1, source_target_pairs={{0,64},{64,128},{128,192},{1,65},{65,129},{129,193},{2,66},{66,130... | collective-permute-start | bytes 49160 | tf_op jit(solution)/shard_map/ppermute | solution.py:418
  41.0 9.5 %copy-start.2 = (f32[4,8,128]{2,1,0:T(8,128)}, f32[4,8,128]{2,1,0:T(8,128)S(1)}, u32[]{:S(2)}) copy-start(f32[4,8,128]{2,1,0:T(8,128)S(1)} %collective-permute-done.1) | copy-start | bytes 49156
  41.0 9.5 %copy-start.3 = (f32[4,8,128]{2,1,0:T(8,128)}, f32[4,8,128]{2,1,0:T(8,128)S(1)}, u32[]{:S(2)}) copy-start(f32[4,8,128]{2,1,0:T(8,128)S(1)} %collective-permute-done) | copy-start | bytes 49156
  50.5 0.8 copy-start
  232.5 28.9 %copy-start.9 = (f32[32,128]{1,0:T(8,128)S(1)}, f32[32,128]{1,0:T(8,128)}, u32[]{:S(2)}) copy-start(f32[32,128]{1,0:T(8,128)} %get-tuple-element.9) | copy-start | bytes 49156
  232.5 30.2 %copy-start.8 = (f32[32,128]{1,0:T(8,128)S(1)}, f32[32,128]{1,0:T(8,128)}, u32[]{:S(2)}) copy-start(f32[32,128]{1,0:T(8,128)} %get-tuple-element.10) | copy-start | bytes 49156
  232.6 45.3 %all-to-all-start.2 = ((f32[64,2,8,128]{3,2,1,0:T(8,128)}), f32[64,2,8,128]{3,2,1,0:T(8,128)S(1)}, u32[]{:S(2)}, u32[]{:S(2)}) async-start(f32[64,2,8,128]{3,2,1,0:T(8,128)} %bitcast.23), calls=%async_computation.2 | async-start | bytes 1048576 | tf_op jit(solution)/shard_map/all_to_all | solution.py:485
  261.4 2.6 collective-permute-start.2
  262.7 5.3 %collective-permute-start.3 = (f32[4,8,128]{2,1,0:T(8,128)S(1)}, f32[4,8,128]{2,1,0:T(8,128)S(1)}, u32[]{:S(2)}, u32[]{:S(2)}) collective-permute-start(f32[4,8,128]{2,1,0:T(8,128)S(1)} %bitcast.27), channel_id=1, source_target_pairs={{64,0},{128,64},{192,128},{65,1},{129,65},{193,129},{66,2},{130,66... | collective-permute-start | bytes 49160 | tf_op jit(solution)/shard_map/ppermute | solution.py:493
  264.0 13.8 %copy-start.4 = (f32[4,8,128]{2,1,0:T(8,128)}, f32[4,8,128]{2,1,0:T(8,128)S(1)}, u32[]{:S(2)}) copy-start(f32[4,8,128]{2,1,0:T(8,128)S(1)} %collective-permute-done.2.low_ref) | copy-start | bytes 49156
  268.1 9.8 %copy-start.5 = (f32[4,8,128]{2,1,0:T(8,128)}, f32[4,8,128]{2,1,0:T(8,128)S(1)}, u32[]{:S(2)}) copy-start(f32[4,8,128]{2,1,0:T(8,128)S(1)} %collective-permute-done.3.high_ref) | copy-start | bytes 49156
  277.9 0.8 copy-start.1
